TPU v7x, 512 devices: a whole 4x8x8 slice. The times are simulated.
512 devices in a mesh: row: 16 (over z, core), col: 16 (over x_hi, y), freq: 2 (over x_lo).
Axes of the slice: x: 4 (x_hi: 2, x_lo: 2; x = x_hi * 2 + x_lo), y: 8, z: 8, core: 2. Of those that a mesh axis runs over, the one named last changes fastest.
Arguments:
- spectra: bfloat16 [10240, 4096], P(('row', 'col'), 'freq'), parts along dimension 1, may hold values from -6 to 6
- loading: float32 [20480], P('freq'), parts along dimension 0, may hold values from 0.05 to 0.5
- delays: int32 [10240, 2048], P('row', 'col'), may hold values from 0 to 1023
- bin_index: int32 [2], P('freq'), parts along dimension 0, may hold values from 1 to 1023
Outputs:
- trailing: float32 [20480, 10240], P(('freq', 'row'), 'col'), parts along dimension 0
- panel: float32 [20480, 512], P(('freq', 'row')), parts along dimension 0
- whitened: float32 [2, 20480, 2048], P(None, ('freq', 'row'), 'col'), parts along dimension 1
There are 2 independent parts, one for each index of `freq`. A program takes and returns all parts, laid end to end along the dimension named above; an argument that names none is the same for every part. Nothing has to cross between parts.
All inputs are finite; a program needn't handle non-finite values.
Results may differ from a plain program's by a relative error of at most 0.0003.
Values may be sent and summed in bfloat16 or wider, within the bound.
A program may use at most 64 MiB of HBM per device.

v0:
```python
import jax
import jax.numpy as jnp
from jax import lax
from jax.sharding import PartitionSpec as P

PANEL = 512
NFFT = 2048


two_pi = 6.283185307179586


def from_root(value, axis, source):
    kept = jnp.where(lax.axis_index(axis) == source, value, 0).astype(value.dtype)
    return lax.psum(kept, axis)


def lower_solve(factor, right_side):
    return jax.scipy.linalg.solve_triangular(factor, right_side, lower=True)


def gram_head(source, loading, snap_count):
    head_csd = jnp.dot(source, source.T, preferred_element_type=jnp.float32) / snap_count
    return jnp.linalg.cholesky(head_csd + jnp.diag(loading[:PANEL]))


def on_device(spectra, loading, delays, bin_index):
    row_index = lax.axis_index("row")
    col_index = lax.axis_index("col")
    tile_size = delays.shape[0]
    slow_count = delays.shape[1]
    snap_count = spectra.shape[1] // 2
    own_rows = lax.all_gather(spectra, "col", axis=0, tiled=True)
    col_rows = from_root(own_rows, "row", col_index)
    row_load = lax.dynamic_slice_in_dim(loading, row_index * tile_size, tile_size)
    tile_csd = jnp.dot(own_rows, col_rows.T, preferred_element_type=jnp.float32) / snap_count
    tile_csd = tile_csd + jnp.where(row_index == col_index, jnp.diag(row_load), 0.0)
    source = jnp.where(row_index == 0, own_rows[:PANEL], col_rows[:PANEL])
    factor = gram_head(source, loading, snap_count)
    own_panel = lower_solve(factor, tile_csd[:, :PANEL].T).T
    own_panel = from_root(own_panel, "col", 0)
    col_panel = from_root(own_panel, "row", col_index)
    glob_rows = row_index * tile_size + jnp.arange(tile_size)
    glob_cols = col_index * tile_size + jnp.arange(tile_size)
    update = tile_csd - jnp.dot(
        own_panel, col_panel.T, precision=lax.Precision.HIGHEST, preferred_element_type=jnp.float32
    )
    keep_mask = (glob_rows[:, None] >= PANEL) & (glob_cols[None, :] >= PANEL)
    trailing = jnp.where(keep_mask, update, 0.0)
    phase_int = delays * bin_index[0] % NFFT
    phase_angle = phase_int.astype(jnp.float32) * (two_pi / NFFT)
    steer_tile = jnp.concatenate([jnp.cos(phase_angle), jnp.sin(phase_angle)], axis=1)
    solved = lower_solve(factor, steer_tile[:PANEL])
    solved = from_root(solved, "row", 0)
    lower_rows = steer_tile - jnp.dot(
        own_panel, solved, precision=lax.Precision.HIGHEST, preferred_element_type=jnp.float32
    )
    padded = jnp.pad(solved, ((0, tile_size - PANEL), (0, 0)))
    stacked = jnp.where(glob_rows[:, None] < PANEL, padded, lower_rows)
    whitened = jnp.stack([stacked[:, :slow_count], stacked[:, slow_count:]])
    return (trailing, own_panel, whitened)


def solution(mesh):
    return jax.shard_map(
        on_device,
        mesh=mesh,
        in_specs=(P(("row", "col"), "freq"), P("freq"), P("row", "col"), P("freq")),
        out_specs=(
            P(("freq", "row"), "col"),
            P(("freq", "row"), None),
            P(None, ("freq", "row"), "col"),
        ),
        check_vma=False,
    )
```

profile of v0, /device:TPU:1, one launch (start us, length us, event | category | flops | bytes accessed | tf_op | source)
XLA Modules:
  0.0 691.1 jit_solution(5855652967183265948)
XLA Ops:
  7.2 0.7 all-gather.2.cloned.1.call-update
  8.0 99.0 %all-gather.2.cloned.1.call-done = bf16[640,2048]{1,0:T(8,128)(2,1)} async-done(((bf16[40,2048]{1,0:T(8,128)(2,1)}), bf16[640,2048]{1,0:T(8,128)(2,1)}) %all-gather.2.cloned.1.call-update) | async-done | bytes 2621456 | tf_op jit(solution)/shard_map/all_gather | solution.py:33
  106.9 1.7 broadcast_select_fusion
  109.6 1.3 fusion.56
  110.9 122.5 %all-reduce.7.cloned.1.call-done = bf16[640,2048]{1,0:T(8,128)(2,1)} async-done(((bf16[640,2048]{1,0:T(8,128)(2,1)}), bf16[640,2048]{1,0:T(8,128)(2,1)}) %all-reduce.7.cloned.1.call-update) | async-done | bytes 2621456 | tf_op jit(solution)/shard_map/psum | solution.py:15
  233.4 4.7 fusion.3
  239.1 1.0 copy-done.2
  240.1 11.7 %cholesky.103 = f32[128,128]{1,0:T(8,128)S(1)} custom-call(f32[128,128]{1,0:T(8,128)S(1)} %cholesky.263), custom_call_target="Cholesky" | custom-call | tf_op jit(solution)/shard_map/jit(cholesky)/cholesky | solution.py:24
  251.8 9.8 %custom-call.34 = f32[1,128,128]{1,2,0:T(8,128)S(1)} custom-call(f32[1,128,128]{2,1,0:T(8,128)S(1)} %get-tuple-element.39), custom_call_target="InvertDiagBlocksLowerTriangular" | custom-call | tf_op jit(solution)/shard_map/jit(cholesky)/cholesky | solution.py:24
  261.8 1.2 constant_dynamic-update-slice_fusion.3
  263.0 1.3 convolution_subtract_fusion.4
  264.3 12.2 %cholesky.215 = f32[128,128]{1,0:T(8,128)S(1)} custom-call(f32[128,128]{1,0:T(8,128)S(1)} %cholesky.267), custom_call_target="Cholesky" | custom-call | tf_op jit(solution)/shard_map/jit(cholesky)/cholesky | solution.py:24
  276.5 9.8 %custom-call.35 = f32[1,128,128]{1,2,0:T(8,128)S(1)} custom-call(f32[1,128,128]{2,1,0:T(8,128)S(1)} %get-tuple-element.36), custom_call_target="InvertDiagBlocksLowerTriangular" | custom-call | tf_op jit(solution)/shard_map/jit(cholesky)/cholesky | solution.py:24
  286.6 1.3 convolution_subtract_fusion.7
  287.9 11.7 %cholesky.236 = f32[128,128]{1,0:T(8,128)S(1)} custom-call(f32[128,128]{1,0:T(8,128)S(1)} %cholesky.272), custom_call_target="Cholesky" | custom-call | tf_op jit(solution)/shard_map/jit(cholesky)/cholesky | solution.py:24
  299.6 0.7 compare_reduce_fusion.1
  300.3 9.8 %custom-call.36 = f32[1,128,128]{1,2,0:T(8,128)S(1)} custom-call(f32[1,128,128]{2,1,0:T(8,128)S(1)} %get-tuple-element.33), custom_call_target="InvertDiagBlocksLowerTriangular" | custom-call | tf_op jit(solution)/shard_map/jit(cholesky)/cholesky | solution.py:24
  310.4 1.2 convolution_subtract_fusion.9
  311.6 11.9 %cholesky.253 = f32[128,128]{1,0:T(8,128)S(1)} custom-call(f32[128,128]{1,0:T(8,128)S(1)} %convolution_subtract_fusion.9), custom_call_target="Cholesky" | custom-call | tf_op jit(solution)/shard_map/jit(cholesky)/cholesky | solution.py:24
  323.5 0.7 compare_reduce_fusion
  324.2 0.6 compare_reduce_fusion.2
  327.6 8.0 %while.1 = (s32[]{:T(128)}, f32[512,512]{1,0:T(8,128)S(1)}, s32[4,2]{0,1:T(2,128)S(1)}, f32[4,128,128]{2,1,0:T(8,128)S(1)}, s32[]{:T(128)}) while((s32[]{:T(128)}, f32[512,512]{1,0:T(8,128)S(1)}, s32[4,2]{0,1:T(2,128)S(1)}, f32[4,128,128]{2,1,0:T(8,128)S(1)}, s32[]{:T(128)}) %tuple.35), condition=%wide.while_cond, body=%wide.while_body.sunk | while | flops 2 | bytes 131189 | solution.py:19
  327.7 0.5 fusion.82
  328.2 1.4 bitcast_dynamic-update-slice_fusion.2
  329.7 0.5 fusion.82
  330.2 1.4 bitcast_dynamic-update-slice_fusion.2
  331.7 0.5 fusion.82
  332.2 1.4 bitcast_dynamic-update-slice_fusion.2
  333.7 0.5 fusion.82
  334.2 1.4 bitcast_dynamic-update-slice_fusion.2
  335.7 39.3 %custom-call.37 = f32[4,128,128]{1,2,0:T(8,128)S(1)} custom-call(f32[4,128,128]{2,1,0:T(8,128)S(1)} %get-tuple-element.10), custom_call_target="InvertDiagBlocksLowerTriangular" | custom-call | tf_op jit(solution)/shard_map/jit(_solve_triangular)/triangular_solve | solution.py:19
  375.0 4.8 bitcast_add_fusion
  380.3 0.6 copy-done.1
  381.8 0.5 convolution_subtract_fusion.1
  382.4 0.5 fusion.51
  382.8 0.9 convolution_subtract_fusion.3
  383.7 0.5 fusion.53
  384.2 1.1 fusion.4
  387.8 0.8 maximum_select_fusion.1
  388.7 150.9 %all-reduce.9.cloned.1.call-done = f32[640,512]{0,1:T(8,128)} async-done(((f32[640,512]{0,1:T(8,128)}), f32[640,512]{0,1:T(8,128)}) %all-reduce.9.cloned.1.call-update) | async-done | bytes 1310736 | tf_op jit(solution)/shard_map/psum | solution.py:15
  539.6 1.2 broadcast_select_fusion.1
  540.8 0.6 copy-done
  541.4 1.5 copy.10
  542.9 129.0 %all-reduce.11.cloned.1.call-done = (f32[640,512]{0,1:T(8,128)}, f32[512,256]{1,0:T(8,128)}) async-done(((f32[640,512]{0,1:T(8,128)}, f32[512,256]{1,0:T(8,128)}), (f32[640,512]{0,1:T(8,128)}, f32[512,256]{1,0:T(8,128)})) %all-reduce.11.cloned.1.call-update) | async-done | bytes 1835024 | tf_op jit(solution)/shard_map/psum | solution.py:15
  671.9 6.5 subtract_select_fusion
  678.4 2.8 copy.9
  681.2 2.2 fusion.5
  683.5 0.9 pad_maximum_fusion.1
  (53 shorter events, 6.4 us)
Async XLA Ops:
  7.2 99.7 %all-gather.2.cloned.1.call-start = ((), (), s32[]{:S(2)}) async-start(), calls=%async_computation | async-start | bytes 2785280 | tf_op jit(solution)/shard_map/all_gather | solution.py:33
  7.9 225.5 %all-reduce.7.cloned.1.call-start = ((), (), s32[]{:S(2)}) async-start(), calls=%async_computation.1 | async-start | bytes 5242880 | tf_op jit(solution)/shard_map/psum | solution.py:15
  108.6 0.8 copy-start.5
  108.6 1.0 copy-start.4
  108.6 431.0 %all-reduce.9.cloned.1.call-start = ((), (), s32[]{:S(2)}) async-start(), calls=%async_computation.2 | async-start | bytes 2621440 | tf_op jit(solution)/shard_map/psum | solution.py:15
  238.2 0.7 slice-start
  239.1 1.0 copy-start.2
  379.7 1.2 copy-start.1
  385.4 286.6 %all-reduce.11.cloned.1.call-start = ((), (), s32[]{:S(2)}) async-start(), calls=%async_computation.3 | async-start | bytes 3670016 | tf_op jit(solution)/shard_map/psum | solution.py:15
  539.6 1.8 copy-start
  678.4 2.8 copy-start.3
Sparse Core Ops, SparseCore 0:
  11.1 95.7 all-gather.1
  109.3 124.1 all-reduce.6
  385.5 154.1 all-reduce.8
  542.5 129.3 all-reduce.10
where the time goes:
time: 701 us; the launch traced here: 691 us
  waiting for transfers between devices  502 us (72%)
  other arithmetic  126 us (18%)
  matrix products  29.6 us (4%)
  between operations  17.7 us (3%)
  local copies, waits for them, and re-layouts  15.4 us (2%)
    psum x3, waiting for transfers between devices, from_root(): return lax.psum(kept, axis)  402 us
    all_gather x1, waiting for transfers between devices, on_device(): own_rows = lax.all_gather(spectra, 'col', axis=0, tiled=True)  99 us
    another operation x14, other arithmetic, gram_head(): return jnp.linalg.cholesky(head_csd + jnp.diag(loading[:PANEL]))  79.1 us
    another operation x3, other arithmetic, lower_solve(): return jax.scipy.linalg.solve_triangular(factor, right_side, lower=True)  39.4 us
  transfers between devices with their start and end apart: 4, of which 4 were waited for; matrix products, arithmetic and copies ran while one was open for 1% of the time, Pallas kernels for 0%

commit v1 on v0

v1 whole, which is shorter than its diff:
```python
import jax
import jax.numpy as jnp
from jax import lax
from jax.experimental import pallas as pl
from jax.experimental.pallas import tpu as pltpu
from jax.sharding import PartitionSpec as P

PANEL = 512
NFFT = 2048
NB = 128
SUB = 40
F32 = jnp.float32
HI = lax.Precision.HIGHEST
MESH = pl.DeviceIdType.MESH
TOP_BLOCKS = 13


def dot_nt(a, b, precision=None):
    return lax.dot_general(
        a, b, (((1,), (1,)), ((), ())), precision=precision, preferred_element_type=F32
    )


def dot_nn(a, b, precision=None):
    return lax.dot_general(
        a, b, (((1,), (0,)), ((), ())), precision=precision, preferred_element_type=F32
    )


def gather_kernel(spec, dly, sr, sc, s0, td, loc, zs, zr, xs, ys, yr, ts, tr, ax, ay, bz, br, bf):
    row = lax.axis_index("row")
    col = lax.axis_index("col")
    z, core = row // 2, row % 2
    xh, y = col // 8, col % 8
    sgn = 1 - 2 * core

    def dev(z_, core_, xh_, y_):
        return {"row": z_ * 2 + core_, "col": xh_ * 8 + y_}

    mate = dev(z, 1 - core, xh, y)
    xmate = dev(z, core, 1 - xh, y)
    yplus = dev(z, core, xh, (y + 1) % 8)
    yminus = dev(z, core, xh, (y + 7) % 8)
    ynext = dev(z, core, xh, (y + sgn + 8) % 8)
    znext = dev((z + sgn + 8) % 8, core, xh, y)
    zprev = dev((z - sgn + 8) % 8, core, xh, y)
    peers = (mate, xmate, yplus, yminus, znext, zprev)

    barrier = pltpu.get_barrier_semaphore()
    for peer in peers:
        pl.semaphore_signal(barrier, inc=1, device_id=peer, device_id_type=MESH)

    drains = []

    def rows(ref, j):
        return ref.at[pl.ds(pl.multiple_of(j * SUB, 8), SUB), :]

    def copy(src, sems, index, target, dst=None):
        return pltpu.make_async_remote_copy(
            src_ref=src,
            dst_ref=src if dst is None else dst,
            send_sem=sems.at[0, index],
            recv_sem=sems.at[1, index],
            device_id=target,
            device_id_type=MESH,
        )

    def send(cond, src, sems, index, target):
        desc = copy(src, sems, index, target)
        if cond is None:
            desc.start()
        else:
            @pl.when(cond)
            def _():
                desc.start()
        drains.append((cond, desc))

    def recv(cond, dst, sems, index):
        desc = copy(dst, sems, index, mate)
        if cond is None:
            desc.wait_recv()
        else:
            @pl.when(cond)
            def _():
                desc.wait_recv()

    own = col
    keep_row = pltpu.make_async_copy(spec, rows(sr, own), loc.at[0])
    keep_row.start()
    is_src = row == 0
    have = own < TOP_BLOCKS
    keep_top = pltpu.make_async_copy(spec, rows(s0, own), loc.at[1])

    @pl.when(is_src & have)
    def _():
        keep_top.start()

    keep_del = pltpu.make_async_copy(dly.at[pl.ds(0, PANEL), :], td, loc.at[2])

    @pl.when(is_src)
    def _():
        keep_del.start()
        keep_del.wait()

    @pl.when(is_src & have)
    def _():
        keep_top.wait()

    keep_row.wait()
    pl.semaphore_wait(barrier, len(peers))

    gets_z = ((core == 0) & (z >= 1) & (z <= 4)) | ((core == 1) & (z >= 5))
    gets_m = jnp.logical_not(is_src | gets_z)
    send_z = ((core == 0) & (z <= 3)) | ((core == 1) & ((z == 0) | (z >= 6)))
    send_m = is_src | gets_z
    for c in range(4):
        piece = s0.at[pl.ds(pl.multiple_of(own * SUB, 8), SUB), pl.ds(c * 512, 512)]
        piece_ok = have
        recv(piece_ok & gets_z, piece, zs, c)
        recv(piece_ok & gets_m, piece, zr, c)
        send(piece_ok & send_z, piece, zs, c, znext)
        send(piece_ok & send_m, piece, zr, c, mate)

    pair = (1 - xh) * 8 + y
    pair_ok = pair < TOP_BLOCKS
    own_top = rows(s0, jnp.minimum(own, TOP_BLOCKS - 1))
    pair_top = rows(s0, jnp.minimum(pair, TOP_BLOCKS - 1))
    send(have, own_top, xs, 0, xmate)
    send(have, own_top, ys, 0, ynext)
    recv(pair_ok, pair_top, xs, 0)
    send(pair_ok, pair_top, ys, 1, ynext)
    steps = 4 - core
    for s in range(1, 5):
        for h in range(2):
            src_xh = xh if h == 0 else 1 - xh
            j = src_xh * 8 + (y - sgn * s + 8) % 8
            ok = (j < TOP_BLOCKS) & (s <= steps)
            part = rows(s0, jnp.minimum(j, TOP_BLOCKS - 1))
            recv(ok, part, ys, 2 * (s - 1) + h)
            if s < 4:
                send(ok & (s < steps), part, ys, 2 * s + h, ynext)
            send(ok, part, yr, 2 * (s - 1) + h, mate)

    own_row = rows(sr, own)
    pair_row = rows(sr, pair)
    send(None, own_row, ax, 0, xmate)
    send(None, own_row, ay, 0, yplus)
    send(None, own_row, ay, 1, yminus)
    recv(None, pair_row, ax, 0)
    send(None, pair_row, ay, 2, yplus)
    send(None, pair_row, ay, 3, yminus)
    for c in range(4):
        piece = td.at[pl.ds(c * 128, 128), :]
        recv(gets_z, piece, ts, c)
        recv(gets_m, piece, tr, c)
        send(send_z, piece, ts, c, znext)
        send(send_m, piece, tr, c, mate)
    for s in range(1, 5):
        for h in range(2):
            src_xh = xh if h == 0 else 1 - xh
            for d, target in ((0, yplus), (1, yminus)):
                if d == 1 and s == 4:
                    continue
                shift = -s if d == 0 else s
                part = rows(sr, src_xh * 8 + (y + shift + 8) % 8)
                index = 4 * (s - 1) + 2 * h + d
                recv(None, part, ay, index)
                if s < 4 - d:
                    send(None, part, ay, index + 4, target)

    zsrc, qsrc = col // 2, col % 2
    at_src = z == zsrc
    is_head = at_src & (core == qsrc)
    is_tail = at_src & (core != qsrc)
    away = jnp.logical_not(at_src)
    far = (sgn * (z - zsrc) + 8) % 8
    whole = pltpu.make_async_copy(sr, sc, loc.at[0])

    @pl.when(is_head)
    def _():
        whole.start()
        whole.wait()

    def half(j, c):
        return sc.at[
            pl.ds(pl.multiple_of(j * SUB, 8), SUB), pl.ds(pl.multiple_of(c * 1024, 1024), 1024)
        ]

    for t in range(16):
        full = rows(sc, t)
        mine = half(t, core)
        send(is_head, full, bf, t, mate)
        recv(is_tail, full, bf, t)
        recv(away, mine, bz, t)
        send(far < 7, mine, bz, t, znext)
        send(away, mine, br, t, mate)

    for s in range(1, 5):
        for h in range(2):
            src_xh = xh if h == 0 else 1 - xh
            j = src_xh * 8 + (y + sgn * s + 8) % 8
            ok = (j < TOP_BLOCKS) & (s <= 3 + core)
            recv(ok, rows(s0, jnp.minimum(j, TOP_BLOCKS - 1)), yr, 2 * (s - 1) + h)
    for t in range(16):
        recv(away, half(t, 1 - core), br, t)
    for cond, desc in drains:
        if cond is None:
            desc.wait_send()
        else:
            @pl.when(cond)
            def _(desc=desc):
                desc.wait_send()


def gather(spectra, delays):
    vmem = pl.BlockSpec(memory_space=pltpu.VMEM)
    dma = pltpu.SemaphoreType.DMA
    return pl.pallas_call(
        gather_kernel,
        out_shape=(
            jax.ShapeDtypeStruct((640, 2048), jnp.bfloat16),
            jax.ShapeDtypeStruct((640, 2048), jnp.bfloat16),
            jax.ShapeDtypeStruct((TOP_BLOCKS * SUB, 2048), jnp.bfloat16),
            jax.ShapeDtypeStruct((PANEL, 128), jnp.int32),
        ),
        in_specs=[vmem] * 2,
        out_specs=(vmem,) * 4,
        scratch_shapes=[
            dma((3,)), dma((2, 4)), dma((2, 4)), dma((2, 1)), dma((2, 8)), dma((2, 8)),
            dma((2, 4)), dma((2, 4)), dma((2, 1)), dma((2, 16)), dma((2, 16)), dma((2, 16)),
            dma((2, 16)),
        ],
        compiler_params=pltpu.CompilerParams(collective_id=0, has_side_effects=True),
        name="gather_blocks",
    )(spectra, delays)


def factor_block(tile):
    lanes = (8, NB)
    sub = lax.broadcasted_iota(jnp.int32, lanes, 0)
    col_id = lax.broadcasted_iota(jnp.int32, (NB, NB), 1)
    row_id = lax.broadcasted_iota(jnp.int32, (NB, NB), 0)
    rest = tile
    aug = jnp.where(row_id == col_id, 1.0, 0.0).astype(F32)
    inverse = []
    for i in range(NB // 8):
        top, eye = rest[:8], aug[:8]
        cols = [jnp.broadcast_to(top[:, 8 * i + b : 8 * i + b + 1], lanes) for b in range(8)]
        scales, rows_t, rows_e, links = [], [], [], []
        for j in range(8):
            scale = lax.rsqrt(jnp.broadcast_to(cols[j][j : j + 1], lanes))
            lower = cols[j] * scale
            below = jnp.where(sub > j, lower, 0.0)
            row_t = jnp.broadcast_to(top[j : j + 1], lanes) * scale
            row_e = jnp.broadcast_to(eye[j : j + 1], lanes) * scale
            top = jnp.where(sub == j, row_t, top - below * row_t)
            eye = jnp.where(sub == j, row_e, eye - below * row_e)
            link = {}
            for b in range(j + 1, 8):
                link[b] = jnp.broadcast_to(lower[b : b + 1], lanes)
                cols[b] = cols[b] - below * link[b]
            scales.append(scale)
            rows_t.append(row_t)
            rows_e.append(row_e)
            links.append(link)
        inverse.append(eye)
        if i == NB // 8 - 1:
            break
        count = NB - 8 * (i + 1)
        rest, aug = rest[8:], aug[8:]
        full = (count, NB)

        def spread(value):
            return jnp.broadcast_to(value[None], (count // 8, 8, NB)).reshape(full)

        parts = [jnp.broadcast_to(rest[:, 8 * i + b : 8 * i + b + 1], full) for b in range(8)]
        for j in range(8):
            lower = parts[j] * spread(scales[j])
            rest = rest - lower * spread(rows_t[j])
            aug = aug - lower * spread(rows_e[j])
            for b in range(j + 1, 8):
                parts[b] = parts[b] - lower * spread(links[j][b])
    return jnp.concatenate(inverse, axis=0)


def factor_kernel(s0, load, low, inv, work):
    head = s0[:PANEL]
    diag = lax.broadcasted_iota(jnp.int32, (PANEL, PANEL), 0) == lax.broadcasted_iota(
        jnp.int32, (PANEL, PANEL), 1
    )
    work[...] = dot_nt(head, head) * (1.0 / 1024) + jnp.where(diag, load[...], 0.0)
    low[...] = jnp.zeros_like(low)

    def step(k, carry):
        at = pl.ds(pl.multiple_of(k * NB, NB), NB)
        inverse = factor_block(work[at, at])
        inv[at, :] = inverse
        panel = dot_nt(work[:, at], inverse, HI)
        below = lax.broadcasted_iota(jnp.int32, (PANEL, NB), 0) >= (k + 1) * NB
        panel = jnp.where(below, panel, 0.0)
        low[:, at] = panel
        work[...] = work[...] - dot_nt(panel, panel, HI)
        return carry

    lax.fori_loop(0, PANEL // NB, step, 0)


def factorize(s0, load):
    vmem = pl.BlockSpec(memory_space=pltpu.VMEM)
    return pl.pallas_call(
        factor_kernel,
        out_shape=(
            jax.ShapeDtypeStruct((PANEL, PANEL), F32),
            jax.ShapeDtypeStruct((PANEL, NB), F32),
        ),
        in_specs=[vmem] * 2,
        out_specs=(vmem,) * 2,
        scratch_shapes=[pltpu.VMEM((PANEL, PANEL), F32)],
        name="factor_head",
    )(s0, load)


def steer_of(delays, bin_value):
    phase = (delays * bin_value) & (NFFT - 1)
    turned = phase + NFFT // 8
    quad = (turned >> 9) & 3
    angle = ((turned & 511) - 256).astype(F32) * (6.283185307179586 / NFFT)
    sq = angle * angle
    cosine = 1.0 + sq * (-0.5 + sq * (1.0 / 24 + sq * (-1.0 / 720 + sq * (1.0 / 40320))))
    sine = angle * (1.0 + sq * (-1.0 / 6 + sq * (1.0 / 120 + sq * (-1.0 / 5040 + sq * (1.0 / 362880)))))
    swap = (quad & 1) == 1
    base_c = jnp.where(swap, sine, cosine)
    base_s = jnp.where(swap, cosine, sine)
    out_c = jnp.where((quad == 1) | (quad == 2), -base_c, base_c)
    out_s = jnp.where(quad >= 2, -base_s, base_s)
    return out_c, out_s


def finish_kernel(spot, bins, sr, sc, s0, low, inv, load_r, load_c, dly, td, trail, panel, white, pc):
    row, col = spot[0], spot[1]
    head = s0[:PANEL]

    def solve_rows(block, load, is_first):
        base = dot_nt(block, head) * (1.0 / 1024)
        diag = lax.broadcasted_iota(jnp.int32, base.shape, 0) == lax.broadcasted_iota(
            jnp.int32, base.shape, 1
        )
        base = base + jnp.where(diag & is_first, load[:, :PANEL], 0.0)
        solved = []
        for k in range(PANEL // NB):
            part = base[:, k * NB : (k + 1) * NB]
            if k:
                known = jnp.concatenate(solved, axis=1)
                part = part - dot_nt(known, low[k * NB : (k + 1) * NB, : k * NB], HI)
            solved.append(dot_nt(part, inv[k * NB : (k + 1) * NB, :], HI))
        return jnp.concatenate(solved, axis=1)

    own = solve_rows(sr[...], load_r[...], row == 0)
    panel[...] = own
    other = solve_rows(sc[...], load_c[...], col == 0)
    shape = (640, 640)
    ids_r = lax.broadcasted_iota(jnp.int32, shape, 0)
    ids_c = lax.broadcasted_iota(jnp.int32, shape, 1)
    tile = dot_nt(sr[...], sc[...]) * (1.0 / 1024)
    tile = tile + jnp.where((ids_r == ids_c) & (row == col), load_r[...], 0.0)
    update = tile - dot_nt(own, other, HI)
    keep = (ids_r + row * 640 >= PANEL) & (ids_c + col * 640 >= PANEL)
    trail[...] = jnp.where(keep, update, 0.0)

    top = jnp.concatenate(steer_of(td[...], bins[0]), axis=1)
    solved = []
    for k in range(PANEL // NB):
        part = top[k * NB : (k + 1) * NB]
        if k:
            known = jnp.concatenate(solved, axis=0)
            part = part - dot_nn(low[k * NB : (k + 1) * NB, : k * NB], known, HI)
        solved.append(dot_nn(inv[k * NB : (k + 1) * NB, :], part, HI))
    solved = jnp.concatenate(solved, axis=0)
    steer = jnp.concatenate(steer_of(dly[...], bins[0]), axis=1)
    lower = steer - dot_nn(own, solved, HI)
    padded = jnp.concatenate([solved, jnp.zeros((640 - PANEL, 256), F32)], axis=0)
    ids = lax.broadcasted_iota(jnp.int32, lower.shape, 0)
    stacked = jnp.where((ids < PANEL) & (row == 0), padded, lower)
    white[0] = stacked[:, :128]
    white[1] = stacked[:, 128:]


def finish(spot, bins, sr, sc, s0, low, inv, load_r, load_c, delays, td):
    vmem = pl.BlockSpec(memory_space=pltpu.VMEM)
    smem = pl.BlockSpec(memory_space=pltpu.SMEM)
    return pl.pallas_call(
        finish_kernel,
        out_shape=(
            jax.ShapeDtypeStruct((640, 640), F32),
            jax.ShapeDtypeStruct((640, PANEL), F32),
            jax.ShapeDtypeStruct((2, 640, 128), F32),
        ),
        in_specs=[smem] * 2 + [vmem] * 9,
        out_specs=(vmem,) * 3,
        scratch_shapes=[pltpu.VMEM((8, 128), F32)],
        name="finish_tiles",
    )(spot, bins, sr, sc, s0, low, inv, load_r, load_c, delays, td)


def on_device(spectra, loading, delays, bin_index):
    row = lax.axis_index("row")
    col = lax.axis_index("col")
    load_r = lax.dynamic_slice_in_dim(loading, row * 640, 640)[None]
    load_c = lax.dynamic_slice_in_dim(loading, col * 640, 640)[None]
    spot = jnp.stack([row, col]).astype(jnp.int32)
    sr, sc, s0, td = gather(spectra, delays)
    low, inv = factorize(s0, loading[None, :PANEL])
    return finish(spot, bin_index, sr, sc, s0, low, inv, load_r, load_c, delays, td)


def solution(mesh):
    return jax.shard_map(
        on_device,
        mesh=mesh,
        in_specs=(P(("row", "col"), "freq"), P("freq"), P("row", "col"), P("freq")),
        out_specs=(
            P(("freq", "row"), "col"),
            P(("freq", "row"), None),
            P(None, ("freq", "row"), "col"),
        ),
        check_vma=False,
    )
```

time: 701 us -> 183 us (0.26)
  the two profiles are of different devices: /device:TPU:1 before, /device:TPU:199 now
where the time goes in v1:
time: 183 us; the launch traced here: 182 us
  Pallas kernels  177 us (97%)
  local copies, waits for them, and re-layouts  3.25 us (2%)
    pallas_call x1, Pallas kernels, gather(): pl.pallas_call(gather_kernel, out_shape=(jax.ShapeDtypeStruct((640, 2048)...  126 us
    pallas_call x1, Pallas kernels, finish(): pl.pallas_call(finish_kernel, out_shape=(jax.ShapeDtypeStruct((640, 640),...  26.3 us
    pallas_call x1, Pallas kernels, factorize(): pl.pallas_call(factor_kernel, out_shape=(jax.ShapeDtypeStruct((PANEL, PAN...  25.3 us

profile of v1, /device:TPU:199, one launch (start us, length us, event | category | flops | bytes accessed | tf_op | source)
XLA Modules:
  0.0 182.4 jit_solution(7594178262695266252)
XLA Ops:
  1.3 0.6 pad_add_fusion.spot
  1.9 1.3 slice.3
  3.2 0.8 fusion
  4.0 0.6 broadcast_in_dim.11.load_c
  4.6 0.5 broadcast_in_dim.10.load_r
  5.1 125.6 %gather_blocks.1 = (bf16[640,2048]{1,0:T(8,128)(2,1)}, bf16[640,2048]{1,0:T(8,128)(2,1)}, bf16[520,2048]{1,0:T(8,128)(2,1)}, s32[512,128]{1,0:T(8,128)}) custom-call(bf16[40,2048]{1,0:T(8,128)(2,1)} %spec.1, s32[640,128]{1,0:T(8,128)} %dly.3), custom_call_target="tpu_custom_call" | custom-call | tf_op jit(solution)/shard_map/gather_blocks/pallas_call | solution.py:218
  130.8 25.3 %factor_head.1 = (f32[512,512]{1,0:T(8,128)}, f32[512,128]{1,0:T(8,128)}) custom-call(bf16[520,2048]{1,0:T(8,128)(2,1)} %get-tuple-element.11.s0, f32[1,512]{1,0:T(1,128)} %bitcast.3), custom_call_target="tpu_custom_call" | custom-call | tf_op jit(solution)/shard_map/factor_head/pallas_call | solution.py:310
  156.1 26.3 %finish_tiles.1 = (f32[640,640]{1,0:T(8,128)}, f32[640,512]{1,0:T(8,128)}, f32[2,640,128]{2,1,0:T(8,128)}) custom-call(s32[2]{0:T(128)} %pad_add_fusion.spot, s32[1]{0:T(128)S(6)} %copy.7.bins, bf16[640,2048]{1,0:T(8,128)(2,1)} %get-tuple-element.9.sr, bf16[640,2048]{1,0:T(8,128)(2,1)} %get-tuple-element.10.sc, bf16[520,2048]{1,0:T(8,128)(2,1)} %get-tuple-element.11.s0, ...), custom_call_target="tpu_custom_call" | custom-call | tf_op jit(solution)/shard_map/finish_tiles/pallas_call | solution.py:391

commit v2 on v1

v2 whole, which is shorter than its diff:
```python
import jax
import jax.numpy as jnp
from jax import lax
from jax.experimental import pallas as pl
from jax.experimental.pallas import tpu as pltpu
from jax.sharding import PartitionSpec as P

PANEL = 512
NFFT = 2048
NB = 128
SUB = 40
F32 = jnp.float32
HI = lax.Precision.HIGHEST
MESH = pl.DeviceIdType.MESH
TOP_BLOCKS = 13
HOLD = 10
SLOTS = 16 + HOLD + 9


def dot_nt(a, b, precision=None):
    return lax.dot_general(
        a, b, (((1,), (1,)), ((), ())), precision=precision, preferred_element_type=F32
    )


def dot_nn(a, b, precision=None):
    return lax.dot_general(
        a, b, (((1,), (0,)), ((), ())), precision=precision, preferred_element_type=F32
    )


def gather_kernel(
    spec, dly, sr, sc, s0, td, loc, rings, top_mate, top_next, top_back, col_mate, col_next, col_back, del_sems
):
    row = lax.axis_index("row")
    col = lax.axis_index("col")
    z, core = row // 2, row % 2
    xh, y = col // 8, col % 8
    sgn = 1 - 2 * core

    def dev(z_, core_, xh_, y_):
        return {"row": z_ * 2 + core_, "col": xh_ * 8 + y_}

    mate = dev(z, 1 - core, xh, y)
    xmate = dev(z, core, 1 - xh, y)
    yplus = dev(z, core, xh, (y + 1) % 8)
    yminus = dev(z, core, xh, (y + 7) % 8)
    znext = dev((z + sgn + 8) % 8, core, xh, y)
    zprev = dev((z - sgn + 8) % 8, core, xh, y)
    peers = (mate, xmate, yplus, yminus, znext, zprev)

    barrier = pltpu.get_barrier_semaphore()
    for peer in peers:
        pl.semaphore_signal(barrier, inc=1, device_id=peer, device_id_type=MESH)

    def block_of(t):
        s, k = (t + 2) // 4, (t + 2) % 4
        d = (k % 2 + k // 2) % 2
        return ((xh + k % 2) % 2) * 8 + (y + (2 * d - 1) * s + 8) % 8, d

    def rows(ref, j):
        return ref.at[pl.ds(pl.multiple_of(j * SUB, 8), SUB), :]

    def half(ref, j, c):
        return ref.at[
            pl.ds(pl.multiple_of(j * SUB, 8), SUB), pl.ds(pl.multiple_of(c * 1024, 1024), 1024)
        ]

    def copy(src, dst, sems, index, target):
        return pltpu.make_async_remote_copy(
            src_ref=src,
            dst_ref=dst,
            send_sem=sems.at[0, index],
            recv_sem=sems.at[1, index],
            device_id=target,
            device_id_type=MESH,
        )

    def both(t, act):
        j, d = block_of(t)
        part = rows(sr, j)

        @pl.when(t == 0)
        def _():
            act(copy(part, part, rings, 1, xmate))
            act(copy(part, part, rings, 2, yplus))
            act(copy(part, part, rings, 4, yminus))

        @pl.when(t == 1)
        def _():
            act(copy(part, part, rings, 3, yminus))
            act(copy(part, part, rings, 5, yplus))

        @pl.when((t >= 2) & (t <= 11))
        def _():
            act(copy(part, part, rings, t + 4, dev(z, core, xh, (y + 1 - 2 * d + 8) % 8)))

    def ring(t):
        j, _ = block_of(t)
        part = rows(sr, j)

        @pl.when((t >= 1) & (t <= 15))
        def _():
            copy(part, part, rings, t, mate).wait_recv()

        both(t, lambda c: c.start())

    class Cast:
        def __init__(self, hold, origin, zsrc, qsrc, sems):
            self.hold, self.origin = hold, origin
            self.to_mate, self.to_next, self.back = sems
            at_src = z == zsrc
            self.head = at_src & (core == qsrc)
            self.tail = at_src & (core != qsrc)
            self.away = jnp.logical_not(at_src)
            self.far = (sgn * (z - zsrc) + 8) % 8

        def sends(self, t, ok, act):
            full_from, full_to, part_from, part_to = self.refs(t)

            @pl.when(ok & self.head)
            def _():
                act(copy(full_from, full_to, self.to_mate, t, mate))
                act(copy(part_from, part_to, self.to_next, t, znext))

            @pl.when(ok & self.tail)
            def _():
                act(copy(part_to, part_to, self.to_next, t, znext))

            @pl.when(ok & self.away)
            def _():
                act(copy(part_to, part_to, self.back, t, mate))

            @pl.when(ok & self.away & (self.far < 7))
            def _():
                act(copy(part_to, part_to, self.to_next, t, znext))

        def refs(self, t):
            j, _ = block_of(t)
            return rows(self.origin, j), rows(self.hold, j), half(self.origin, j, core), half(self.hold, j, core)

        def other(self, t):
            return half(self.hold, block_of(t)[0], 1 - core)

        def step(self, t, ok):
            _, full, _, part = self.refs(t)

            @pl.when(ok & self.tail)
            def _():
                copy(full, full, self.to_mate, t, mate).wait_recv()

            @pl.when(ok & self.away)
            def _():
                copy(part, part, self.to_next, t, mate).wait_recv()

            self.sends(t, ok, lambda c: c.start())

        def collect(self, t, ok):
            part = self.other(t)

            @pl.when(ok & self.away)
            def _():
                copy(part, part, self.back, t, mate).wait_recv()

    class DelayCast(Cast):
        def refs(self, t):
            mine = pl.ds(pl.multiple_of(core * 256, 256), 256)
            return self.hold, self.hold, self.hold.at[mine, :], self.hold.at[mine, :]

        def other(self, t):
            return self.hold.at[pl.ds(pl.multiple_of((1 - core) * 256, 256), 256), :]

    top = Cast(s0, sr, 0, 0, (top_mate, top_next, top_back))
    side = Cast(sc, sr, col // 2, col % 2, (col_mate, col_next, col_back))
    turns = DelayCast(td, td, 0, 0, (del_sems.at[0], del_sems.at[1], del_sems.at[2]))

    def top_ok(t):
        return (t >= 0) & (t <= 15) & (block_of(t)[0] < TOP_BLOCKS)

    def side_ok(t):
        return (t >= 0) & (t <= 15)

    keep_row = pltpu.make_async_copy(spec, rows(sr, col), loc.at[0])
    keep_row.start()
    keep_del = pltpu.make_async_copy(dly.at[pl.ds(0, PANEL), :], td, loc.at[1])

    @pl.when(row == 0)
    def _():
        keep_del.start()
        keep_del.wait()

    keep_row.wait()
    pl.semaphore_wait(barrier, len(peers))

    late = HOLD * ((row == 1).astype(jnp.int32))
    slow = HOLD * ((col == 1).astype(jnp.int32))
    fast = (row == 0).astype(jnp.int32)
    top_lag = jnp.minimum(z, 1) * (top.far + 1)
    side_lag = slow + side.away.astype(jnp.int32) * (side.far + 2)
    turn_at = 2 * turns.far + 2

    def slot(n, carry):
        at = (1 + fast) * (n - late)
        ring(at)
        ring((at + 2) * fast - 1)
        first = 2 * (n - top_lag)
        top.step(first, top_ok(first))
        top.step(first + 1, top_ok(first + 1))
        turns.step(0, n == turn_at)
        t = n - side_lag
        side.step(t, side_ok(t))
        return carry

    lax.fori_loop(0, SLOTS, slot, 0)

    def tidy(t, carry):
        top.collect(t, top_ok(t))
        side.collect(t, side_ok(t))
        both(t, lambda c: c.wait_send())
        top.sends(t, top_ok(t), lambda c: c.wait_send())
        side.sends(t, side_ok(t), lambda c: c.wait_send())
        return carry

    turns.collect(0, row >= 0)
    turns.sends(0, row >= 0, lambda c: c.wait_send())
    lax.fori_loop(0, 16, tidy, 0)
    keep_top = pltpu.make_async_copy(sr.at[pl.ds(0, TOP_BLOCKS * SUB), :], s0, loc.at[0])
    keep_col = pltpu.make_async_copy(sr, sc, loc.at[1])

    @pl.when(top.head)
    def _():
        keep_top.start()
        keep_top.wait()

    @pl.when(side.head)
    def _():
        keep_col.start()
        keep_col.wait()


def gather(spectra, delays):
    vmem = pl.BlockSpec(memory_space=pltpu.VMEM)
    dma = pltpu.SemaphoreType.DMA
    return pl.pallas_call(
        gather_kernel,
        out_shape=(
            jax.ShapeDtypeStruct((640, 2048), jnp.bfloat16),
            jax.ShapeDtypeStruct((640, 2048), jnp.bfloat16),
            jax.ShapeDtypeStruct((TOP_BLOCKS * SUB, 2048), jnp.bfloat16),
            jax.ShapeDtypeStruct((PANEL, 128), jnp.int32),
        ),
        in_specs=[vmem] * 2,
        out_specs=(vmem,) * 4,
        scratch_shapes=[dma((2,))] + [dma((2, 16))] * 7 + [dma((3, 2, 1))],
        compiler_params=pltpu.CompilerParams(collective_id=0, has_side_effects=True),
        name="gather_blocks",
    )(spectra, delays)


def factor_block(tile):
    lanes = (8, NB)
    sub = lax.broadcasted_iota(jnp.int32, lanes, 0)
    col_id = lax.broadcasted_iota(jnp.int32, (NB, NB), 1)
    row_id = lax.broadcasted_iota(jnp.int32, (NB, NB), 0)
    rest = tile
    aug = jnp.where(row_id == col_id, 1.0, 0.0).astype(F32)
    inverse = []
    for i in range(NB // 8):
        top, eye = rest[:8], aug[:8]
        cols = [jnp.broadcast_to(top[:, 8 * i + b : 8 * i + b + 1], lanes) for b in range(8)]
        scales, rows_t, rows_e, links = [], [], [], []
        for j in range(8):
            scale = lax.rsqrt(jnp.broadcast_to(cols[j][j : j + 1], lanes))
            lower = cols[j] * scale
            below = jnp.where(sub > j, lower, 0.0)
            row_t = jnp.broadcast_to(top[j : j + 1], lanes) * scale
            row_e = jnp.broadcast_to(eye[j : j + 1], lanes) * scale
            top = jnp.where(sub == j, row_t, top - below * row_t)
            eye = jnp.where(sub == j, row_e, eye - below * row_e)
            link = {}
            for b in range(j + 1, 8):
                link[b] = jnp.broadcast_to(lower[b : b + 1], lanes)
                cols[b] = cols[b] - below * link[b]
            scales.append(scale)
            rows_t.append(row_t)
            rows_e.append(row_e)
            links.append(link)
        inverse.append(eye)
        if i == NB // 8 - 1:
            break
        count = NB - 8 * (i + 1)
        rest, aug = rest[8:], aug[8:]
        full = (count, NB)

        def spread(value):
            return jnp.broadcast_to(value[None], (count // 8, 8, NB)).reshape(full)

        parts = [jnp.broadcast_to(rest[:, 8 * i + b : 8 * i + b + 1], full) for b in range(8)]
        for j in range(8):
            lower = parts[j] * spread(scales[j])
            rest = rest - lower * spread(rows_t[j])
            aug = aug - lower * spread(rows_e[j])
            for b in range(j + 1, 8):
                parts[b] = parts[b] - lower * spread(links[j][b])
    return jnp.concatenate(inverse, axis=0)


def factor_kernel(s0, load, low, inv, work):
    head = s0[:PANEL]
    ids = lax.broadcasted_iota(jnp.int32, (PANEL, PANEL), 0)
    diag = ids == lax.broadcasted_iota(jnp.int32, (PANEL, PANEL), 1)
    lane = jnp.concatenate([load[b : b + 1, :] for b in range(PANEL // NB)], axis=1)
    work[...] = dot_nt(head, head) * (1.0 / 1024) + jnp.where(diag, lane, 0.0)
    low[...] = jnp.zeros_like(low)
    inv[...] = jnp.zeros_like(inv)

    def step(k, carry):
        at = pl.ds(pl.multiple_of(k * NB, NB), NB)
        inverse = factor_block(work[at, at])
        inv[at, pl.ds(pl.multiple_of((k % 2) * NB, NB), NB)] = inverse
        panel = dot_nt(work[:, at], inverse, HI)
        below = lax.broadcasted_iota(jnp.int32, (PANEL, NB), 0) >= (k + 1) * NB
        panel = jnp.where(below, panel, 0.0)
        low[:, at] = panel
        work[...] = work[...] - dot_nt(panel, panel, HI)
        return carry

    lax.fori_loop(0, PANEL // NB, step, 0)
    for q in range(2):
        a, b, c = 2 * q * NB, (2 * q + 1) * NB, (2 * q + 2) * NB
        inner = dot_nn(low[b:c, a:b], inv[a:b, :NB], HI)
        inv[b:c, :NB] = -dot_nn(inv[b:c, NB:], inner, HI)


def factorize(s0, load):
    vmem = pl.BlockSpec(memory_space=pltpu.VMEM)
    return pl.pallas_call(
        factor_kernel,
        out_shape=(
            jax.ShapeDtypeStruct((PANEL, PANEL), F32),
            jax.ShapeDtypeStruct((PANEL, 2 * NB), F32),
        ),
        in_specs=[vmem] * 2,
        out_specs=(vmem,) * 2,
        scratch_shapes=[pltpu.VMEM((PANEL, PANEL), F32)],
        name="factor_head",
    )(s0, load)


def split(value):
    high = value.astype(jnp.bfloat16)
    return high, (value - high.astype(F32)).astype(jnp.bfloat16)


def three(dot, a, b):
    return dot(a[0], b[0]) + (dot(a[0], b[1]) + dot(a[1], b[0]))


def steer_of(delays, bin_value):
    phase = (delays * bin_value) & (NFFT - 1)
    turned = phase + NFFT // 8
    quad = (turned >> 9) & 3
    angle = ((turned & 511) - 256).astype(F32) * (6.283185307179586 / NFFT)
    sq = angle * angle
    cosine = 1.0 + sq * (-0.5 + sq * (1.0 / 24 + sq * (-1.0 / 720 + sq * (1.0 / 40320))))
    sine = angle * (1.0 + sq * (-1.0 / 6 + sq * (1.0 / 120 + sq * (-1.0 / 5040 + sq * (1.0 / 362880)))))
    swap = (quad & 1) == 1
    base_c = jnp.where(swap, sine, cosine)
    base_s = jnp.where(swap, cosine, sine)
    out_c = jnp.where((quad == 1) | (quad == 2), -base_c, base_c)
    out_s = jnp.where(quad >= 2, -base_s, base_s)
    return out_c, out_s


def finish_kernel(bins, sr, sc, s0, low, inv, load, dly, td, trail, panel, white):
    row, col = lax.axis_index("row"), lax.axis_index("col")
    head = s0[:PANEL]
    mid = 2 * NB
    inv_a, inv_b = split(inv[:mid]), split(inv[mid:])
    link = split(low[mid:, :mid])

    def lanes_of(index):
        return jnp.concatenate([load[pl.ds(index * 5 + b, 1), :] for b in range(5)], axis=1)

    def solve_rows(block, lane, is_first):
        base = dot_nt(block, head) * (1.0 / 1024)
        ids = lax.broadcasted_iota(jnp.int32, base.shape, 0)
        diag = ids == lax.broadcasted_iota(jnp.int32, base.shape, 1)
        base = base + jnp.where(diag & is_first, lane[:, :PANEL], 0.0)
        left = three(dot_nt, split(base[:, :mid]), inv_a)
        left_parts = split(left)
        right = base[:, mid:] - three(dot_nt, left_parts, link)
        right = three(dot_nt, split(right), inv_b)
        right_parts = split(right)
        whole = [jnp.concatenate([p, q], axis=1) for p, q in zip(left_parts, right_parts)]
        return jnp.concatenate([left, right], axis=1), whole

    lane_r = lanes_of(row)
    own, own_parts = solve_rows(sr[...], lane_r, row == 0)
    panel[...] = own
    _, other_parts = solve_rows(sc[...], lanes_of(col), col == 0)
    shape = (640, 640)
    ids_r = lax.broadcasted_iota(jnp.int32, shape, 0)
    ids_c = lax.broadcasted_iota(jnp.int32, shape, 1)
    tile = dot_nt(sr[...], sc[...]) * (1.0 / 1024)
    tile = tile + jnp.where((ids_r == ids_c) & (row == col), lane_r, 0.0)
    update = tile - three(dot_nt, own_parts, other_parts)
    keep = (ids_r + row * 640 >= PANEL) & (ids_c + col * 640 >= PANEL)
    trail[...] = jnp.where(keep, update, 0.0)

    upper = jnp.concatenate(steer_of(td[...], bins[0]), axis=1)
    first = three(dot_nn, inv_a, split(upper[:mid]))
    second = upper[mid:] - three(dot_nn, link, split(first))
    second = three(dot_nn, inv_b, split(second))
    solved = jnp.concatenate([first, second], axis=0)
    steer = jnp.concatenate(steer_of(dly[...], bins[0]), axis=1)
    lower = steer - three(dot_nn, own_parts, split(solved))
    padded = jnp.concatenate([solved, jnp.zeros((640 - PANEL, 256), F32)], axis=0)
    ids = lax.broadcasted_iota(jnp.int32, lower.shape, 0)
    stacked = jnp.where((ids < PANEL) & (row == 0), padded, lower)
    white[0] = stacked[:, :128]
    white[1] = stacked[:, 128:]


def finish(bins, sr, sc, s0, low, inv, load, delays, td):
    vmem = pl.BlockSpec(memory_space=pltpu.VMEM)
    smem = pl.BlockSpec(memory_space=pltpu.SMEM)
    return pl.pallas_call(
        finish_kernel,
        out_shape=(
            jax.ShapeDtypeStruct((640, 640), F32),
            jax.ShapeDtypeStruct((640, PANEL), F32),
            jax.ShapeDtypeStruct((2, 640, 128), F32),
        ),
        in_specs=[smem] + [vmem] * 8,
        out_specs=(vmem,) * 3,
        name="finish_tiles",
    )(bins, sr, sc, s0, low, inv, load, delays, td)


def on_device(spectra, loading, delays, bin_index):
    load = loading.reshape(80, 128)
    sr, sc, s0, td = gather(spectra, delays)
    low, inv = factorize(s0, load)
    return finish(bin_index, sr, sc, s0, low, inv, load, delays, td)


def solution(mesh):
    return jax.shard_map(
        on_device,
        mesh=mesh,
        in_specs=(P(("row", "col"), "freq"), P("freq"), P("row", "col"), P("freq")),
        out_specs=(
            P(("freq", "row"), "col"),
            P(("freq", "row"), None),
            P(None, ("freq", "row"), "col"),
        ),
        check_vma=False,
    )
```

time: 183 us -> 142 us (0.78)
  the two profiles are of different devices: /device:TPU:199 before, /device:TPU:25 now
where the time goes in v2:
time: 142 us
  Pallas kernels  140 us (99%)
    pallas_call x1, Pallas kernels, gather(): pl.pallas_call(gather_kernel, out_shape=(jax.ShapeDtypeStruct((640, 2048)...  98.7 us
    pallas_call x1, Pallas kernels, factorize(): pl.pallas_call(factor_kernel, out_shape=(jax.ShapeDtypeStruct((PANEL, PAN...  26.7 us
    pallas_call x1, Pallas kernels, finish(): pl.pallas_call(finish_kernel, out_shape=(jax.ShapeDtypeStruct((640, 640),...  15 us

profile of v2, /device:TPU:25, one launch (start us, length us, event | category | flops | bytes accessed | tf_op | source)
XLA Modules:
  0.0 141.6 jit_solution(10828378727535388100)
XLA Ops:
  1.3 98.7 %gather_blocks.1 = (bf16[640,2048]{1,0:T(8,128)(2,1)}, bf16[640,2048]{1,0:T(8,128)(2,1)}, bf16[520,2048]{1,0:T(8,128)(2,1)}, s32[512,128]{1,0:T(8,128)}) custom-call(bf16[40,2048]{1,0:T(8,128)(2,1)} %spec.1, s32[640,128]{1,0:T(8,128)} %dly.3), custom_call_target="tpu_custom_call" | custom-call | tf_op jit(solution)/shard_map/gather_blocks/pallas_call | solution.py:244
  100.0 26.7 %factor_head.1 = (f32[512,512]{1,0:T(8,128)}, f32[512,256]{1,0:T(8,128)}) custom-call(bf16[520,2048]{1,0:T(8,128)(2,1)} %get-tuple-element.11.s0, f32[80,128]{1,0:T(8,128)} %bitcast.1), custom_call_target="tpu_custom_call" | custom-call | tf_op jit(solution)/shard_map/factor_head/pallas_call | solution.py:337
  126.7 15.0 %finish_tiles.1 = (f32[640,640]{1,0:T(8,128)}, f32[640,512]{1,0:T(8,128)}, f32[2,640,128]{2,1,0:T(8,128)}) custom-call(s32[1]{0:T(128)S(6)} %copy.7.bins, bf16[640,2048]{1,0:T(8,128)(2,1)} %get-tuple-element.9.sr, bf16[640,2048]{1,0:T(8,128)(2,1)} %get-tuple-element.10.sc, bf16[520,2048]{1,0:T(8,128)(2,1)} %get-tuple-element.11.s0, ...), custom_call_target="tpu_custom_call" | custom-call | tf_op jit(solution)/shard_map/finish_tiles/pallas_call | solution.py:428

commit v3 on v2

--- a/solution.py
+++ b/solution.py
@@ -13,8 +13,8 @@
 HI = lax.Precision.HIGHEST
 MESH = pl.DeviceIdType.MESH
 TOP_BLOCKS = 13
-HOLD = 10
-SLOTS = 16 + HOLD + 9
+HOLD = 14
+LEAD = 30
 
 
 def dot_nt(a, b, precision=None):
@@ -30,7 +30,8 @@
 
 
 def gather_kernel(
-    spec, dly, sr, sc, s0, td, loc, rings, top_mate, top_next, top_back, col_mate, col_next, col_back, del_sems
+    spec, dly, load, sr, sc, s0, td, low, inv, work, loc, rings, top_mate, top_next, top_back,
+    col_mate, col_next, col_back, del_mate, del_next, del_back
 ):
     row = lax.axis_index("row")
     col = lax.axis_index("col")
@@ -163,22 +164,28 @@
                 copy(part, part, self.back, t, mate).wait_recv()
 
     class DelayCast(Cast):
+        def piece(self, t, c):
+            return self.hold.at[pl.ds(pl.multiple_of(t * 256 + c * 128, 128), 128), :]
+
         def refs(self, t):
-            mine = pl.ds(pl.multiple_of(core * 256, 256), 256)
-            return self.hold, self.hold, self.hold.at[mine, :], self.hold.at[mine, :]
+            full = self.hold.at[pl.ds(pl.multiple_of(t * 256, 256), 256), :]
+            return full, full, self.piece(t, core), self.piece(t, core)
 
         def other(self, t):
-            return self.hold.at[pl.ds(pl.multiple_of((1 - core) * 256, 256), 256), :]
+            return self.piece(t, 1 - core)
 
     top = Cast(s0, sr, 0, 0, (top_mate, top_next, top_back))
     side = Cast(sc, sr, col // 2, col % 2, (col_mate, col_next, col_back))
-    turns = DelayCast(td, td, 0, 0, (del_sems.at[0], del_sems.at[1], del_sems.at[2]))
+    turns = DelayCast(td, td, 0, 0, (del_mate, del_next, del_back))
 
     def top_ok(t):
         return (t >= 0) & (t <= 15) & (block_of(t)[0] < TOP_BLOCKS)
 
     def side_ok(t):
         return (t >= 0) & (t <= 15)
+
+    def turn_ok(t):
+        return (t >= 0) & (t <= 1)
 
     keep_row = pltpu.make_async_copy(spec, rows(sr, col), loc.at[0])
     keep_row.start()
@@ -192,72 +199,69 @@
     keep_row.wait()
     pl.semaphore_wait(barrier, len(peers))
 
-    late = HOLD * ((row == 1).astype(jnp.int32))
-    slow = HOLD * ((col == 1).astype(jnp.int32))
-    fast = (row == 0).astype(jnp.int32)
-    top_lag = jnp.minimum(z, 1) * (top.far + 1)
-    side_lag = slow + side.away.astype(jnp.int32) * (side.far + 2)
-    turn_at = 2 * turns.far + 2
-
-    def slot(n, carry):
-        at = (1 + fast) * (n - late)
-        ring(at)
-        ring((at + 2) * fast - 1)
-        first = 2 * (n - top_lag)
-        top.step(first, top_ok(first))
-        top.step(first + 1, top_ok(first + 1))
-        turns.step(0, n == turn_at)
-        t = n - side_lag
+    def ring_slot(n):
+        late = n - HOLD
+
+        @pl.when(row == 0)
+        def _():
+            ring(n)
+
+        @pl.when((row == 1) & (late % 2 == 0))
+        def _():
+            ring(late // 2)
+
+        @pl.when((row >= 2) & ((2 * n) % 5 < 2))
+        def _():
+            ring((2 * n) // 5)
+
+    def lead_slot(n, carry):
+        ring_slot(n)
+        t = n - 2 * top.far
+        top.step(t, top_ok(t))
+        return carry
+
+    def side_slot(n):
+        ring_slot(n)
+        t = n - LEAD - 2 * side.far
         side.step(t, side_ok(t))
+        t = n - LEAD - 16 - 2 * turns.far
+        turns.step(t, turn_ok(t))
+
+    lax.fori_loop(0, LEAD, lead_slot, 0)
+
+    def top_in(t, carry):
+        top.collect(t, top_ok(t))
         return carry
 
-    lax.fori_loop(0, SLOTS, slot, 0)
-
-    def tidy(t, carry):
-        top.collect(t, top_ok(t))
-        side.collect(t, side_ok(t))
-        both(t, lambda c: c.wait_send())
-        top.sends(t, top_ok(t), lambda c: c.wait_send())
-        side.sends(t, side_ok(t), lambda c: c.wait_send())
-        return carry
-
-    turns.collect(0, row >= 0)
-    turns.sends(0, row >= 0, lambda c: c.wait_send())
-    lax.fori_loop(0, 16, tidy, 0)
+    lax.fori_loop(0, 16, top_in, 0)
     keep_top = pltpu.make_async_copy(sr.at[pl.ds(0, TOP_BLOCKS * SUB), :], s0, loc.at[0])
-    keep_col = pltpu.make_async_copy(sr, sc, loc.at[1])
 
     @pl.when(top.head)
     def _():
         keep_top.start()
         keep_top.wait()
 
+    factor(s0, load, low, inv, work, lambda k, i: side_slot(LEAD + 8 * k + i))
+    keep_col = pltpu.make_async_copy(sr, sc, loc.at[1])
+
     @pl.when(side.head)
     def _():
         keep_col.start()
         keep_col.wait()
 
-
-def gather(spectra, delays):
-    vmem = pl.BlockSpec(memory_space=pltpu.VMEM)
-    dma = pltpu.SemaphoreType.DMA
-    return pl.pallas_call(
-        gather_kernel,
-        out_shape=(
-            jax.ShapeDtypeStruct((640, 2048), jnp.bfloat16),
-            jax.ShapeDtypeStruct((640, 2048), jnp.bfloat16),
-            jax.ShapeDtypeStruct((TOP_BLOCKS * SUB, 2048), jnp.bfloat16),
-            jax.ShapeDtypeStruct((PANEL, 128), jnp.int32),
-        ),
-        in_specs=[vmem] * 2,
-        out_specs=(vmem,) * 4,
-        scratch_shapes=[dma((2,))] + [dma((2, 16))] * 7 + [dma((3, 2, 1))],
-        compiler_params=pltpu.CompilerParams(collective_id=0, has_side_effects=True),
-        name="gather_blocks",
-    )(spectra, delays)
-
-
-def factor_block(tile):
+    def tidy(t, carry):
+        side.collect(t, t >= 0)
+        both(t, lambda c: c.wait_send())
+        top.sends(t, top_ok(t), lambda c: c.wait_send())
+        side.sends(t, t >= 0, lambda c: c.wait_send())
+        turns.collect(t, turn_ok(t))
+        turns.sends(t, turn_ok(t), lambda c: c.wait_send())
+        return carry
+
+    lax.fori_loop(0, 16, tidy, 0)
+
+
+def factor_block(tile, between):
     lanes = (8, NB)
     sub = lax.broadcasted_iota(jnp.int32, lanes, 0)
     col_id = lax.broadcasted_iota(jnp.int32, (NB, NB), 1)
@@ -286,6 +290,8 @@
             rows_e.append(row_e)
             links.append(link)
         inverse.append(eye)
+        if i % 2 == 1:
+            between(i // 2)
         if i == NB // 8 - 1:
             break
         count = NB - 8 * (i + 1)
@@ -305,7 +311,7 @@
     return jnp.concatenate(inverse, axis=0)
 
 
-def factor_kernel(s0, load, low, inv, work):
+def factor(s0, load, low, inv, work, between):
     head = s0[:PANEL]
     ids = lax.broadcasted_iota(jnp.int32, (PANEL, PANEL), 0)
     diag = ids == lax.broadcasted_iota(jnp.int32, (PANEL, PANEL), 1)
@@ -316,7 +322,7 @@
 
     def step(k, carry):
         at = pl.ds(pl.multiple_of(k * NB, NB), NB)
-        inverse = factor_block(work[at, at])
+        inverse = factor_block(work[at, at], lambda i: between(k, i))
         inv[at, pl.ds(pl.multiple_of((k % 2) * NB, NB), NB)] = inverse
         panel = dot_nt(work[:, at], inverse, HI)
         below = lax.broadcasted_iota(jnp.int32, (PANEL, NB), 0) >= (k + 1) * NB
@@ -332,19 +338,29 @@
         inv[b:c, :NB] = -dot_nn(inv[b:c, NB:], inner, HI)
 
 
-def factorize(s0, load):
+def gather(spectra, delays, load):
     vmem = pl.BlockSpec(memory_space=pltpu.VMEM)
+    dma = pltpu.SemaphoreType.DMA
     return pl.pallas_call(
-        factor_kernel,
+        gather_kernel,
         out_shape=(
+            jax.ShapeDtypeStruct((640, 2048), jnp.bfloat16),
+            jax.ShapeDtypeStruct((640, 2048), jnp.bfloat16),
+            jax.ShapeDtypeStruct((TOP_BLOCKS * SUB, 2048), jnp.bfloat16),
+            jax.ShapeDtypeStruct((PANEL, 128), jnp.int32),
             jax.ShapeDtypeStruct((PANEL, PANEL), F32),
             jax.ShapeDtypeStruct((PANEL, 2 * NB), F32),
         ),
-        in_specs=[vmem] * 2,
-        out_specs=(vmem,) * 2,
-        scratch_shapes=[pltpu.VMEM((PANEL, PANEL), F32)],
-        name="factor_head",
-    )(s0, load)
+        in_specs=[vmem] * 3,
+        out_specs=(vmem,) * 6,
+        scratch_shapes=[pltpu.VMEM((PANEL, PANEL), F32), dma((2,))]
+        + [dma((2, 16))] * 7
+        + [dma((2, 2))] * 3,
+        compiler_params=pltpu.CompilerParams(
+            collective_id=0, has_side_effects=True, vmem_limit_bytes=20 << 20
+        ),
+        name="gather_and_factor",
+    )(spectra, delays, load)
 
 
 def split(value):
@@ -434,14 +450,14 @@
         ),
         in_specs=[smem] + [vmem] * 8,
         out_specs=(vmem,) * 3,
+        compiler_params=pltpu.CompilerParams(vmem_limit_bytes=36 << 20),
         name="finish_tiles",
     )(bins, sr, sc, s0, low, inv, load, delays, td)
 
 
 def on_device(spectra, loading, delays, bin_index):
     load = loading.reshape(80, 128)
-    sr, sc, s0, td = gather(spectra, delays)
-    low, inv = factorize(s0, load)
+    sr, sc, s0, td, low, inv = gather(spectra, delays, load)
     return finish(bin_index, sr, sc, s0, low, inv, load, delays, td)
 
 

time: 142 us -> 134 us (0.944)
  the two profiles are of different devices: /device:TPU:25 before, /device:TPU:89 now
where the time goes in v3:
time: 134 us
  Pallas kernels  128 us (96%)
  local copies, waits for them, and re-layouts  4.41 us (3%)
    pallas_call x1, Pallas kernels, gather(): pl.pallas_call(gather_kernel, out_shape=(jax.ShapeDtypeStruct((640, 2048)...  117 us
    pallas_call x1, Pallas kernels, finish(): pl.pallas_call(finish_kernel, out_shape=(jax.ShapeDtypeStruct((640, 640),...  11.3 us
    unnamed x10, local copies, waits for them, and re-layouts  4.41 us

profile of v3, /device:TPU:89, one launch (start us, length us, event | category | flops | bytes accessed | tf_op | source)
XLA Modules:
  0.0 134.1 jit_solution(9843734880037294044)
XLA Ops:
  1.3 0.0 copy-start
  1.3 1.0 copy-done
  2.3 0.0 copy-start.2
  2.3 0.9 copy-done.2
  3.2 0.0 copy-start.3
  3.2 0.8 copy-done.3
  3.9 117.1 %gather_and_factor.1 = (bf16[640,2048]{1,0:T(8,128)(2,1)S(1)}, bf16[640,2048]{1,0:T(8,128)(2,1)S(1)}, bf16[520,2048]{1,0:T(8,128)(2,1)S(1)}, s32[512,128]{1,0:T(...) custom-call(bf16[40,2048]{1,0:T(8,128)(2,1)S(1)} %copy-done.2, s32[640,128]{1,0:T(8,128)S(1)} %copy-done, ...), custom_call_target="tpu_custom_call" | custom-call | tf_op jit(solution)/shard_map/gather_and_factor/pallas_call | solution.py:344
  121.0 0.0 copy-start.1
  121.1 1.0 copy-done.1
  122.0 0.0 copy-start.4
  122.0 0.8 copy-done.4
  122.8 11.3 %finish_tiles.1 = (f32[640,640]{1,0:T(8,128)}, f32[640,512]{1,0:T(8,128)}, f32[2,640,128]{2,1,0:T(8,128)}) custom-call(s32[1]{0:T(128)S(6)} %copy.7.bins, bf16[640,2048]{1,0:T(8,128)(2,1)S(1)} %get-tuple-element.9.sr, bf16[640,2048]{1,0:T(8,128)(2,1)S(1)} %get-tuple-element.10.sc, bf16[520,2048]{1,0:T(8,128)(2,1)S(1)} %get-tuple-element.11.s0, ...), custom_call_target="tpu_custom_call" | custom-call | tf_op jit(solution)/shard_map/finish_tiles/pallas_call | solution.py:444
Async XLA Ops:
  1.3 1.0 copy-start
  2.3 0.9 copy-start.2
  3.2 0.8 copy-start.3
  121.0 1.0 copy-start.1
  122.0 0.8 copy-start.4

commit v4 on v3

--- a/solution.py
+++ b/solution.py
@@ -30,8 +30,8 @@
 
 
 def gather_kernel(
-    spec, dly, load, sr, sc, s0, td, low, inv, work, loc, rings, top_mate, top_next, top_back,
-    col_mate, col_next, col_back, del_mate, del_next, del_back
+    spec, dly, load, sr, sc, s0, td, link, inv, low, work, ld, loc, rings, top_mate, top_next, top_back,
+    col_mate, col_plus, col_minus, col_back, del_mate, del_next, del_back, res
 ):
     row = lax.axis_index("row")
     col = lax.axis_index("col")
@@ -46,9 +46,20 @@
     xmate = dev(z, core, 1 - xh, y)
     yplus = dev(z, core, xh, (y + 1) % 8)
     yminus = dev(z, core, xh, (y + 7) % 8)
+    zplus = dev((z + 1) % 8, core, xh, y)
+    zminus = dev((z + 7) % 8, core, xh, y)
     znext = dev((z + sgn + 8) % 8, core, xh, y)
-    zprev = dev((z - sgn + 8) % 8, core, xh, y)
-    peers = (mate, xmate, yplus, yminus, znext, zprev)
+    peers = (mate, xmate, yplus, yminus, zplus, zminus)
+
+    keep_row = pltpu.make_async_copy(spec, sr.at[pl.ds(pl.multiple_of(col * SUB, 8), SUB), :], loc.at[0])
+    keep_row.start()
+    keep_del = pltpu.make_async_copy(dly.at[pl.ds(0, PANEL), :], td, loc.at[1])
+    keep_load = pltpu.make_async_copy(load, ld, loc.at[2])
+    keep_load.start()
+
+    @pl.when(row == 0)
+    def _():
+        keep_del.start()
 
     barrier = pltpu.get_barrier_semaphore()
     for peer in peers:
@@ -106,6 +117,10 @@
 
         both(t, lambda c: c.start())
 
+        @pl.when((t >= 0) & (t <= 15) & (row == col))
+        def _():
+            copy(part, rows(sc, j), col_mate, t, mate).start()
+
     class Cast:
         def __init__(self, hold, origin, zsrc, qsrc, sems):
             self.hold, self.origin = hold, origin
@@ -175,27 +190,65 @@
             return self.piece(t, 1 - core)
 
     top = Cast(s0, sr, 0, 0, (top_mate, top_next, top_back))
-    side = Cast(sc, sr, col // 2, col % 2, (col_mate, col_next, col_back))
     turns = DelayCast(td, td, 0, 0, (del_mate, del_next, del_back))
+
+    zsrc, from_zero = col // 2, col % 2 == 0
+    at_src = z == zsrc
+    caster = at_src & (core == 1)
+    guest = jnp.logical_not(at_src) & (core == 1)
+    far_plus = (z - zsrc + 8) % 8
+    far_minus = (zsrc - z + 8) % 8
+
+    def side_sends(t, ok, way, act):
+        j, _ = block_of(t)
+        sems, target, far = ((col_plus, zplus, far_plus), (col_minus, zminus, far_minus))[way]
+        part = half(sc, j, way)
+
+        @pl.when(ok & caster & from_zero)
+        def _():
+            act(copy(part, part, sems, t, target))
+
+        @pl.when(ok & caster & jnp.logical_not(from_zero))
+        def _():
+            act(copy(half(sr, j, way), part, sems, t, target))
+
+        @pl.when(ok & guest & (far < 7))
+        def _():
+            act(copy(part, part, sems, t, target))
+
+        @pl.when(ok & guest)
+        def _():
+            act(copy(part, part, col_back, 2 * t + way, mate))
+
+    def side_step(m):
+        full = rows(sc, block_of(m)[0])
+
+        @pl.when(caster & from_zero & (m <= 15))
+        def _():
+            copy(full, full, col_mate, m, mate).wait_recv()
+
+        for way, (sems, far) in enumerate(((col_plus, far_plus), (col_minus, far_minus))):
+            t = m - 2 * far
+            ok = (t >= 0) & (t <= 15)
+            part = half(sc, block_of(t)[0], way)
+
+            @pl.when(ok & guest)
+            def _():
+                copy(part, part, sems, t, mate).wait_recv()
+
+            side_sends(t, ok, way, lambda c: c.start())
 
     def top_ok(t):
         return (t >= 0) & (t <= 15) & (block_of(t)[0] < TOP_BLOCKS)
 
-    def side_ok(t):
-        return (t >= 0) & (t <= 15)
-
     def turn_ok(t):
         return (t >= 0) & (t <= 1)
 
-    keep_row = pltpu.make_async_copy(spec, rows(sr, col), loc.at[0])
-    keep_row.start()
-    keep_del = pltpu.make_async_copy(dly.at[pl.ds(0, PANEL), :], td, loc.at[1])
-
     @pl.when(row == 0)
     def _():
-        keep_del.start()
         keep_del.wait()
 
+    keep_load.wait()
     keep_row.wait()
     pl.semaphore_wait(barrier, len(peers))
 
@@ -218,14 +271,8 @@
         ring_slot(n)
         t = n - 2 * top.far
         top.step(t, top_ok(t))
+        turns.step(t, turn_ok(t))
         return carry
-
-    def side_slot(n):
-        ring_slot(n)
-        t = n - LEAD - 2 * side.far
-        side.step(t, side_ok(t))
-        t = n - LEAD - 16 - 2 * turns.far
-        turns.step(t, turn_ok(t))
 
     lax.fori_loop(0, LEAD, lead_slot, 0)
 
@@ -241,21 +288,72 @@
         keep_top.start()
         keep_top.wait()
 
-    factor(s0, load, low, inv, work, lambda k, i: side_slot(LEAD + 8 * k + i))
+    upper, under = pl.ds(0, 2 * NB), pl.ds(2 * NB, 2 * NB)
+    results = [
+        copy(link, link, res, 0, mate),
+        copy(inv.at[upper, :], inv.at[upper, :], res, 1, mate),
+        copy(inv.at[under, :], inv.at[under, :], res, 2, mate),
+    ]
+
+    def col_in(t, carry):
+        j, _ = block_of(t)
+        full = rows(sc, j)
+
+        @pl.when(at_src & jnp.logical_not(from_zero))
+        def _():
+            copy(full, full, col_mate, t, mate).wait_recv()
+
+        @pl.when(jnp.logical_not(at_src))
+        def _():
+            for way in range(2):
+                part = half(sc, j, way)
+                copy(part, part, col_back, 2 * t + way, mate).wait_recv()
+
+        return carry
+
+    @pl.when(core == 0)
+    def _():
+        factor(
+            s0, ld, low, link, inv, work,
+            lambda k, i: ring_slot(LEAD + 8 * k + i),
+            lambda: [c.start() for c in results[:2]],
+        )
+        lax.fori_loop(0, 16, col_in, 0)
+        results[2].start()
+        for c in results:
+            c.wait_send()
+
+    @pl.when(core == 1)
+    def _():
+        def side_slot(m, carry):
+            ring_slot(LEAD + m)
+            side_step(m)
+            return carry
+
+        lax.fori_loop(0, 30, side_slot, 0)
+        for c in results:
+            c.wait_recv()
+
     keep_col = pltpu.make_async_copy(sr, sc, loc.at[1])
 
-    @pl.when(side.head)
+    @pl.when(row == col)
     def _():
         keep_col.start()
         keep_col.wait()
 
     def tidy(t, carry):
-        side.collect(t, t >= 0)
+        j, _ = block_of(t)
         both(t, lambda c: c.wait_send())
         top.sends(t, top_ok(t), lambda c: c.wait_send())
-        side.sends(t, t >= 0, lambda c: c.wait_send())
+        for way in range(2):
+            side_sends(t, t >= 0, way, lambda c: c.wait_send())
         turns.collect(t, turn_ok(t))
         turns.sends(t, turn_ok(t), lambda c: c.wait_send())
+
+        @pl.when(row == col)
+        def _():
+            copy(rows(sr, j), rows(sc, j), col_mate, t, mate).wait_send()
+
         return carry
 
     lax.fori_loop(0, 16, tidy, 0)
@@ -311,14 +409,18 @@
     return jnp.concatenate(inverse, axis=0)
 
 
-def factor(s0, load, low, inv, work, between):
+def factor(s0, load, low, link, inv, work, between, halfway):
     head = s0[:PANEL]
     ids = lax.broadcasted_iota(jnp.int32, (PANEL, PANEL), 0)
     diag = ids == lax.broadcasted_iota(jnp.int32, (PANEL, PANEL), 1)
     lane = jnp.concatenate([load[b : b + 1, :] for b in range(PANEL // NB)], axis=1)
     work[...] = dot_nt(head, head) * (1.0 / 1024) + jnp.where(diag, lane, 0.0)
-    low[...] = jnp.zeros_like(low)
     inv[...] = jnp.zeros_like(inv)
+
+    def join(q):
+        a, b, c = 2 * q * NB, (2 * q + 1) * NB, (2 * q + 2) * NB
+        inner = dot_nn(low[b:c, a:b], inv[a:b, :NB], HI)
+        inv[b:c, :NB] = -dot_nn(inv[b:c, NB:], inner, HI)
 
     def step(k, carry):
         at = pl.ds(pl.multiple_of(k * NB, NB), NB)
@@ -329,17 +431,25 @@
         panel = jnp.where(below, panel, 0.0)
         low[:, at] = panel
         work[...] = work[...] - dot_nt(panel, panel, HI)
+
+        @pl.when(k == 1)
+        def _():
+            join(0)
+            link[...] = low[2 * NB :, : 2 * NB]
+
+        @pl.when(k == 2)
+        def _():
+            halfway()
+
         return carry
 
     lax.fori_loop(0, PANEL // NB, step, 0)
-    for q in range(2):
-        a, b, c = 2 * q * NB, (2 * q + 1) * NB, (2 * q + 2) * NB
-        inner = dot_nn(low[b:c, a:b], inv[a:b, :NB], HI)
-        inv[b:c, :NB] = -dot_nn(inv[b:c, NB:], inner, HI)
+    join(1)
 
 
 def gather(spectra, delays, load):
     vmem = pl.BlockSpec(memory_space=pltpu.VMEM)
+    outside = pl.BlockSpec(memory_space=pltpu.HBM)
     dma = pltpu.SemaphoreType.DMA
     return pl.pallas_call(
         gather_kernel,
@@ -348,14 +458,17 @@
             jax.ShapeDtypeStruct((640, 2048), jnp.bfloat16),
             jax.ShapeDtypeStruct((TOP_BLOCKS * SUB, 2048), jnp.bfloat16),
             jax.ShapeDtypeStruct((PANEL, 128), jnp.int32),
-            jax.ShapeDtypeStruct((PANEL, PANEL), F32),
+            jax.ShapeDtypeStruct((2 * NB, 2 * NB), F32),
             jax.ShapeDtypeStruct((PANEL, 2 * NB), F32),
         ),
-        in_specs=[vmem] * 3,
+        in_specs=[outside] * 3,
         out_specs=(vmem,) * 6,
-        scratch_shapes=[pltpu.VMEM((PANEL, PANEL), F32), dma((2,))]
+        scratch_shapes=[pltpu.VMEM((PANEL, PANEL), F32)] * 2
+        + [pltpu.VMEM((80, 128), F32), dma((3,))]
         + [dma((2, 16))] * 7
-        + [dma((2, 2))] * 3,
+        + [dma((2, 32))]
+        + [dma((2, 2))] * 3
+        + [dma((2, 3))],
         compiler_params=pltpu.CompilerParams(
             collective_id=0, has_side_effects=True, vmem_limit_bytes=20 << 20
         ),
@@ -388,12 +501,20 @@
     return out_c, out_s
 
 
-def finish_kernel(bins, sr, sc, s0, low, inv, load, dly, td, trail, panel, white):
+def finish_kernel(bins, sr, sc, s0, low, inv, load_far, dly_far, td, trail, panel, white, load, dly, sems):
+    fetch = [
+        pltpu.make_async_copy(load_far, load, sems.at[0]),
+        pltpu.make_async_copy(dly_far, dly, sems.at[1]),
+    ]
+    for c in fetch:
+        c.start()
     row, col = lax.axis_index("row"), lax.axis_index("col")
     head = s0[:PANEL]
     mid = 2 * NB
     inv_a, inv_b = split(inv[:mid]), split(inv[mid:])
-    link = split(low[mid:, :mid])
+    link = split(low[...])
+    for c in fetch:
+        c.wait()
 
     def lanes_of(index):
         return jnp.concatenate([load[pl.ds(index * 5 + b, 1), :] for b in range(5)], axis=1)
@@ -441,6 +562,7 @@
 def finish(bins, sr, sc, s0, low, inv, load, delays, td):
     vmem = pl.BlockSpec(memory_space=pltpu.VMEM)
     smem = pl.BlockSpec(memory_space=pltpu.SMEM)
+    outside = pl.BlockSpec(memory_space=pltpu.HBM)
     return pl.pallas_call(
         finish_kernel,
         out_shape=(
@@ -448,8 +570,11 @@
             jax.ShapeDtypeStruct((640, PANEL), F32),
             jax.ShapeDtypeStruct((2, 640, 128), F32),
         ),
-        in_specs=[smem] + [vmem] * 8,
+        in_specs=[smem] + [vmem] * 5 + [outside] * 2 + [vmem],
         out_specs=(vmem,) * 3,
+        scratch_shapes=[
+            pltpu.VMEM((80, 128), F32), pltpu.VMEM((640, 128), jnp.int32), pltpu.SemaphoreType.DMA((2,)),
+        ],
         compiler_params=pltpu.CompilerParams(vmem_limit_bytes=36 << 20),
         name="finish_tiles",
     )(bins, sr, sc, s0, low, inv, load, delays, td)

time: 134 us -> 122 us (0.910)
  the two profiles are of different devices: /device:TPU:89 before, /device:TPU:63 now
where the time goes in v4:
time: 122 us; the launch traced here: 121 us
  Pallas kernels  115 us (94%)
  local copies, waits for them, and re-layouts  4.41 us (4%)
  between operations  1.47 us (1%)
    pallas_call x1, Pallas kernels, gather(): pl.pallas_call(gather_kernel, out_shape=(jax.ShapeDtypeStruct((640, 2048)...  103 us
    pallas_call x1, Pallas kernels, finish(): pl.pallas_call(finish_kernel, out_shape=(jax.ShapeDtypeStruct((640, 640),...  12.1 us
    unnamed x10, local copies, waits for them, and re-layouts  4.41 us

profile of v4, /device:TPU:63, one launch (start us, length us, event | category | flops | bytes accessed | tf_op | source)
XLA Modules:
  0.0 121.4 jit_solution(2832927628432747771)
XLA Ops:
  1.3 0.0 copy-start
  1.3 1.0 copy-done
  2.3 0.0 copy-start.2
  2.3 0.8 copy-done.2
  3.0 0.0 copy-start.4
  3.0 0.9 copy-done.4
  3.9 103.4 %gather_and_factor.1 = (bf16[640,2048]{1,0:T(8,128)(2,1)S(1)}, bf16[640,2048]{1,0:T(8,128)(2,1)S(1)}, bf16[520,2048]{1,0:T(8,128)(2,1)S(1)}, s32[512,128]{1,0:T(...) custom-call(bf16[40,2048]{1,0:T(8,128)(2,1)S(1)} %copy-done.4, s32[640,128]{1,0:T(8,128)S(1)} %copy-done, ...), custom_call_target="tpu_custom_call" | custom-call | tf_op jit(solution)/shard_map/gather_and_factor/pallas_call | solution.py:454
  107.3 0.0 copy-start.1
  107.3 1.0 copy-done.1
  108.3 0.0 copy-start.3
  108.3 0.8 copy-done.3
  109.1 12.1 %finish_tiles.1 = (f32[640,640]{1,0:T(8,128)}, f32[640,512]{1,0:T(8,128)}, f32[2,640,128]{2,1,0:T(8,128)}) custom-call(s32[1]{0:T(128)S(6)} %copy.7.bins, bf16[640,2048]{1,0:T(8,128)(2,1)S(1)} %get-tuple-element.9.sr, bf16[640,2048]{1,0:T(8,128)(2,1)S(1)} %get-tuple-element.10.sc, bf16[520,2048]{1,0:T(8,128)(2,1)S(1)} %get-tuple-element.11.s0, ...), custom_call_target="tpu_custom_call" | custom-call | tf_op jit(solution)/shard_map/finish_tiles/pallas_call | solution.py:566
Async XLA Ops:
  1.3 1.0 copy-start
  2.3 0.8 copy-start.2
  3.0 0.9 copy-start.4
  107.3 1.0 copy-start.1
  108.3 0.8 copy-start.3

commit v5 on v4

--- a/solution.py
+++ b/solution.py
@@ -13,8 +13,9 @@
 HI = lax.Precision.HIGHEST
 MESH = pl.DeviceIdType.MESH
 TOP_BLOCKS = 13
-HOLD = 14
-LEAD = 30
+HOLD = 12
+LEAD = 24
+SIDE = 17
 
 
 def dot_nt(a, b, precision=None):
@@ -189,7 +190,52 @@
         def other(self, t):
             return self.piece(t, 1 - core)
 
-    top = Cast(s0, sr, 0, 0, (top_mate, top_next, top_back))
+    class HeadCast(Cast):
+        def setup(self):
+            limit = 4 - core
+            self.member = self.away & (self.far <= limit)
+            self.onward = self.away & (self.far < limit)
+            self.guest = self.away & (self.far > limit)
+
+        def sends(self, t, ok, act):
+            j, _ = block_of(t)
+            origin, part = rows(self.origin, j), rows(self.hold, j)
+
+            @pl.when(ok & self.head)
+            def _():
+                act(copy(origin, part, self.to_next, t, znext))
+                act(copy(origin, part, self.to_mate, t, mate))
+
+            @pl.when(ok & (self.tail | self.onward))
+            def _():
+                act(copy(part, part, self.to_next, t, znext))
+
+            @pl.when(ok & self.member)
+            def _():
+                act(copy(part, part, self.back, t, mate))
+
+        def step(self, t, ok):
+            part = rows(self.hold, block_of(t)[0])
+
+            @pl.when(ok & self.tail)
+            def _():
+                copy(part, part, self.to_mate, t, mate).wait_recv()
+
+            @pl.when(ok & self.member)
+            def _():
+                copy(part, part, self.to_next, t, mate).wait_recv()
+
+            self.sends(t, ok, lambda c: c.start())
+
+        def collect(self, t, ok):
+            part = rows(self.hold, block_of(t)[0])
+
+            @pl.when(ok & self.guest)
+            def _():
+                copy(part, part, self.back, t, mate).wait_recv()
+
+    top = HeadCast(s0, sr, 0, 0, (top_mate, top_next, top_back))
+    top.setup()
     turns = DelayCast(td, td, 0, 0, (del_mate, del_next, del_back))
 
     zsrc, from_zero = col // 2, col % 2 == 0
@@ -223,7 +269,7 @@
     def side_step(m):
         full = rows(sc, block_of(m)[0])
 
-        @pl.when(caster & from_zero & (m <= 15))
+        @pl.when(caster & from_zero & (m >= 0) & (m <= 15))
         def _():
             copy(full, full, col_mate, m, mate).wait_recv()
 
@@ -259,19 +305,27 @@
         def _():
             ring(n)
 
-        @pl.when((row == 1) & (late % 2 == 0))
-        def _():
-            ring(late // 2)
-
-        @pl.when((row >= 2) & ((2 * n) % 5 < 2))
-        def _():
-            ring((2 * n) // 5)
+        @pl.when((row == 1) & ((2 * late) % 3 < 2))
+        def _():
+            ring((2 * late) // 3)
+
+        @pl.when((row >= 2) & ((3 * n) % 5 < 3))
+        def _():
+            ring((3 * n) // 5)
+
+    slow = 3 * (col == 1).astype(jnp.int32)
 
     def lead_slot(n, carry):
         ring_slot(n)
         t = n - 2 * top.far
         top.step(t, top_ok(t))
+        t = n - 2 * turns.far
         turns.step(t, turn_ok(t))
+
+        @pl.when((core == 1) & (n >= SIDE))
+        def _():
+            side_step(n - SIDE - slow)
+
         return carry
 
     lax.fori_loop(0, LEAD, lead_slot, 0)
@@ -280,7 +334,10 @@
         top.collect(t, top_ok(t))
         return carry
 
-    lax.fori_loop(0, 16, top_in, 0)
+    @pl.when(core == 0)
+    def _():
+        lax.fori_loop(0, 16, top_in, 0)
+
     keep_top = pltpu.make_async_copy(sr.at[pl.ds(0, TOP_BLOCKS * SUB), :], s0, loc.at[0])
 
     @pl.when(top.head)
@@ -311,6 +368,22 @@
 
         return carry
 
+    def drain(t, carry):
+        j, _ = block_of(t)
+        both(t, lambda c: c.wait_send())
+        top.sends(t, top_ok(t), lambda c: c.wait_send())
+
+        @pl.when(turn_ok(t))
+        def _():
+            turns.collect(t, t >= 0)
+            turns.sends(t, t >= 0, lambda c: c.wait_send())
+
+        @pl.when(row == col)
+        def _():
+            copy(rows(sr, j), rows(sc, j), col_mate, t, mate).wait_send()
+
+        return carry
+
     @pl.when(core == 0)
     def _():
         factor(
@@ -318,19 +391,22 @@
             lambda k, i: ring_slot(LEAD + 8 * k + i),
             lambda: [c.start() for c in results[:2]],
         )
+        lax.fori_loop(0, 16, drain, 0)
+        results[2].start()
         lax.fori_loop(0, 16, col_in, 0)
-        results[2].start()
         for c in results:
             c.wait_send()
 
     @pl.when(core == 1)
     def _():
         def side_slot(m, carry):
-            ring_slot(LEAD + m)
-            side_step(m)
+            ring_slot(m)
+            side_step(m - SIDE - slow)
             return carry
 
-        lax.fori_loop(0, 30, side_slot, 0)
+        lax.fori_loop(LEAD, SIDE + 33, side_slot, 0)
+        lax.fori_loop(0, 16, drain, 0)
+        lax.fori_loop(0, 16, top_in, 0)
         for c in results:
             c.wait_recv()
 
@@ -341,22 +417,14 @@
         keep_col.start()
         keep_col.wait()
 
-    def tidy(t, carry):
-        j, _ = block_of(t)
-        both(t, lambda c: c.wait_send())
-        top.sends(t, top_ok(t), lambda c: c.wait_send())
-        for way in range(2):
-            side_sends(t, t >= 0, way, lambda c: c.wait_send())
-        turns.collect(t, turn_ok(t))
-        turns.sends(t, turn_ok(t), lambda c: c.wait_send())
-
-        @pl.when(row == col)
-        def _():
-            copy(rows(sr, j), rows(sc, j), col_mate, t, mate).wait_send()
-
-        return carry
-
-    lax.fori_loop(0, 16, tidy, 0)
+    @pl.when(core == 1)
+    def _():
+        def tidy(t, carry):
+            for way in range(2):
+                side_sends(t, t >= 0, way, lambda c: c.wait_send())
+            return carry
+
+        lax.fori_loop(0, 16, tidy, 0)
 
 
 def factor_block(tile, between):
@@ -581,7 +649,9 @@
 
 
 def on_device(spectra, loading, delays, bin_index):
-    load = loading.reshape(80, 128)
+    load = pltpu.with_memory_space_constraint(loading.reshape(80, 128), pltpu.HBM)
+    spectra = pltpu.with_memory_space_constraint(spectra, pltpu.HBM)
+    delays = pltpu.with_memory_space_constraint(delays, pltpu.HBM)
     sr, sc, s0, td, low, inv = gather(spectra, delays, load)
     return finish(bin_index, sr, sc, s0, low, inv, load, delays, td)
 

time: 122 us -> 113 us (0.926)
  the two profiles are of different devices: /device:TPU:63 before, /device:TPU:297 now
where the time goes in v5:
time: 113 us
  Pallas kernels  111 us (98%)
  between operations  1.45 us (1%)
    pallas_call x1, Pallas kernels, gather(): pl.pallas_call(gather_kernel, out_shape=(jax.ShapeDtypeStruct((640, 2048)...  98.6 us
    pallas_call x1, Pallas kernels, finish(): pl.pallas_call(finish_kernel, out_shape=(jax.ShapeDtypeStruct((640, 640),...  12.7 us

profile of v5, /device:TPU:297, one launch (start us, length us, event | category | flops | bytes accessed | tf_op | source)
XLA Modules:
  0.0 112.7 jit_solution(8848928192110077092)
XLA Ops:
  1.3 98.6 %gather_and_factor.1 = (bf16[640,2048]{1,0:T(8,128)(2,1)S(1)}, bf16[640,2048]{1,0:T(8,128)(2,1)S(1)}, bf16[520,2048]{1,0:T(8,128)(2,1)S(1)}, s32[512,128]{1,0:T(...) custom-call(bf16[40,2048]{1,0:T(8,128)(2,1)} %spec.1, s32[640,128]{1,0:T(8,128)} %dly_far.1, f32[80,128]{1,0:T(8,128)} %bitcast.1), custom_call_target="tpu_custom_call" | custom-call | tf_op jit(solution)/shard_map/gather_and_factor/pallas_call | solution.py:522
  99.9 12.7 %finish_tiles.1 = (f32[640,640]{1,0:T(8,128)}, f32[640,512]{1,0:T(8,128)}, f32[2,640,128]{2,1,0:T(8,128)}) custom-call(s32[1]{0:T(128)S(6)} %copy.7.bins, bf16[640,2048]{1,0:T(8,128)(2,1)S(1)} %get-tuple-element.9.sr, bf16[640,2048]{1,0:T(8,128)(2,1)S(1)} %get-tuple-element.10.sc, bf16[520,2048]{1,0:T(8,128)(2,1)S(1)} %get-tuple-element.11.s0, ...), custom_call_target="tpu_custom_call" | custom-call | tf_op jit(solution)/shard_map/finish_tiles/pallas_call | solution.py:634

commit v6 on v5

--- a/solution.py
+++ b/solution.py
@@ -313,7 +313,8 @@
         def _():
             ring((3 * n) // 5)
 
-    slow = 3 * (col == 1).astype(jnp.int32)
+    held = (zsrc >= 1) & (zsrc <= 3)
+    side_at = SIDE + 3 * (col == 1).astype(jnp.int32) + (LEAD - SIDE) * held.astype(jnp.int32)
 
     def lead_slot(n, carry):
         ring_slot(n)
@@ -324,7 +325,7 @@
 
         @pl.when((core == 1) & (n >= SIDE))
         def _():
-            side_step(n - SIDE - slow)
+            side_step(n - side_at)
 
         return carry
 
@@ -401,12 +402,20 @@
     def _():
         def side_slot(m, carry):
             ring_slot(m)
-            side_step(m - SIDE - slow)
+            side_step(m - side_at)
             return carry
 
-        lax.fori_loop(LEAD, SIDE + 33, side_slot, 0)
+        @pl.when(caster & held)
+        def _():
+            lax.fori_loop(0, 16, top_in, 0)
+
+        lax.fori_loop(LEAD, LEAD + 31, side_slot, 0)
         lax.fori_loop(0, 16, drain, 0)
-        lax.fori_loop(0, 16, top_in, 0)
+
+        @pl.when(jnp.logical_not(caster & held))
+        def _():
+            lax.fori_loop(0, 16, top_in, 0)
+
         for c in results:
             c.wait_recv()
 
@@ -494,11 +503,14 @@
         at = pl.ds(pl.multiple_of(k * NB, NB), NB)
         inverse = factor_block(work[at, at], lambda i: between(k, i))
         inv[at, pl.ds(pl.multiple_of((k % 2) * NB, NB), NB)] = inverse
-        panel = dot_nt(work[:, at], inverse, HI)
-        below = lax.broadcasted_iota(jnp.int32, (PANEL, NB), 0) >= (k + 1) * NB
-        panel = jnp.where(below, panel, 0.0)
-        low[:, at] = panel
-        work[...] = work[...] - dot_nt(panel, panel, HI)
+        for now in range(PANEL // NB - 1):
+            here, rest = slice(now * NB, (now + 1) * NB), slice((now + 1) * NB, PANEL)
+
+            @pl.when(k == now)
+            def _():
+                panel = dot_nt(work[rest, here], inverse, HI)
+                low[rest, here] = panel
+                work[rest, rest] = work[rest, rest] - dot_nt(panel, panel, HI)
 
         @pl.when(k == 1)
         def _():
@@ -581,8 +593,7 @@
     mid = 2 * NB
     inv_a, inv_b = split(inv[:mid]), split(inv[mid:])
     link = split(low[...])
-    for c in fetch:
-        c.wait()
+    fetch[0].wait()
 
     def lanes_of(index):
         return jnp.concatenate([load[pl.ds(index * 5 + b, 1), :] for b in range(5)], axis=1)
@@ -618,6 +629,7 @@
     second = upper[mid:] - three(dot_nn, link, split(first))
     second = three(dot_nn, inv_b, split(second))
     solved = jnp.concatenate([first, second], axis=0)
+    fetch[1].wait()
     steer = jnp.concatenate(steer_of(dly[...], bins[0]), axis=1)
     lower = steer - three(dot_nn, own_parts, split(solved))
     padded = jnp.concatenate([solved, jnp.zeros((640 - PANEL, 256), F32)], axis=0)

time: 113 us -> 109 us (0.965)
  the two profiles are of different devices: /device:TPU:297 before, /device:TPU:177 now
where the time goes in v6:
time: 109 us
  Pallas kernels  107 us (98%)
  between operations  1.45 us (1%)
    pallas_call x1, Pallas kernels, gather(): pl.pallas_call(gather_kernel, out_shape=(jax.ShapeDtypeStruct((640, 2048)...  94.4 us
    pallas_call x1, Pallas kernels, finish(): pl.pallas_call(finish_kernel, out_shape=(jax.ShapeDtypeStruct((640, 640),...  12.8 us

profile of v6, /device:TPU:177, one launch (start us, length us, event | category | flops | bytes accessed | tf_op | source)
XLA Modules:
  0.0 108.7 jit_solution(15070198116713849764)
XLA Ops:
  1.3 94.4 %gather_and_factor.1 = (bf16[640,2048]{1,0:T(8,128)(2,1)S(1)}, bf16[640,2048]{1,0:T(8,128)(2,1)S(1)}, bf16[520,2048]{1,0:T(8,128)(2,1)S(1)}, s32[512,128]{1,0:T(...) custom-call(bf16[40,2048]{1,0:T(8,128)(2,1)} %spec.1, s32[640,128]{1,0:T(8,128)} %dly_far.1, f32[80,128]{1,0:T(8,128)} %bitcast.1), custom_call_target="tpu_custom_call" | custom-call | tf_op jit(solution)/shard_map/gather_and_factor/pallas_call | solution.py:534
  95.7 12.8 %finish_tiles.1 = (f32[640,640]{1,0:T(8,128)}, f32[640,512]{1,0:T(8,128)}, f32[2,640,128]{2,1,0:T(8,128)}) custom-call(s32[1]{0:T(128)S(6)} %copy.7.bins, bf16[640,2048]{1,0:T(8,128)(2,1)S(1)} %get-tuple-element.9.sr, bf16[640,2048]{1,0:T(8,128)(2,1)S(1)} %get-tuple-element.10.sc, bf16[520,2048]{1,0:T(8,128)(2,1)S(1)} %get-tuple-element.11.s0, ...), custom_call_target="tpu_custom_call" | custom-call | tf_op jit(solution)/shard_map/finish_tiles/pallas_call | solution.py:646

commit v7 on v6

--- a/solution.py
+++ b/solution.py
@@ -31,7 +31,7 @@
 
 
 def gather_kernel(
-    spec, dly, load, sr, sc, s0, td, link, inv, low, work, ld, loc, rings, top_mate, top_next, top_back,
+    spec, dly, load, sr, sc, s0, td, link, inv, ld, low, work, loc, rings, top_mate, top_next, top_back,
     col_mate, col_plus, col_minus, col_back, del_mate, del_next, del_back, res
 ):
     row = lax.axis_index("row")
@@ -89,34 +89,35 @@
             device_id_type=MESH,
         )
 
-    def both(t, act):
+    def both(t, q, act):
         j, d = block_of(t)
-        part = rows(sr, j)
+        part = half(sr, j, q)
 
         @pl.when(t == 0)
         def _():
-            act(copy(part, part, rings, 1, xmate))
-            act(copy(part, part, rings, 2, yplus))
-            act(copy(part, part, rings, 4, yminus))
+            act(copy(part, part, rings, 2 + q, xmate))
+            act(copy(part, part, rings, 4 + q, yplus))
+            act(copy(part, part, rings, 8 + q, yminus))
 
         @pl.when(t == 1)
         def _():
-            act(copy(part, part, rings, 3, yminus))
-            act(copy(part, part, rings, 5, yplus))
+            act(copy(part, part, rings, 6 + q, yminus))
+            act(copy(part, part, rings, 10 + q, yplus))
 
         @pl.when((t >= 2) & (t <= 11))
         def _():
-            act(copy(part, part, rings, t + 4, dev(z, core, xh, (y + 1 - 2 * d + 8) % 8)))
+            act(copy(part, part, rings, 2 * t + 8 + q, dev(z, core, xh, (y + 1 - 2 * d + 8) % 8)))
 
     def ring(t):
         j, _ = block_of(t)
+        for q in range(2):
+            @pl.when((t >= 1) & (t <= 15))
+            def _():
+                copy(half(sr, j, q), half(sr, j, q), rings, 2 * t + q, mate).wait_recv()
+
+            both(t, q, lambda c: c.start())
+
         part = rows(sr, j)
-
-        @pl.when((t >= 1) & (t <= 15))
-        def _():
-            copy(part, part, rings, t, mate).wait_recv()
-
-        both(t, lambda c: c.start())
 
         @pl.when((t >= 0) & (t <= 15) & (row == col))
         def _():
@@ -197,42 +198,45 @@
             self.onward = self.away & (self.far < limit)
             self.guest = self.away & (self.far > limit)
 
-        def sends(self, t, ok, act):
+        def sends(self, t, ok, act, q):
             j, _ = block_of(t)
-            origin, part = rows(self.origin, j), rows(self.hold, j)
+            origin, part = half(self.origin, j, q), half(self.hold, j, q)
+            at = 2 * t + q
 
             @pl.when(ok & self.head)
             def _():
-                act(copy(origin, part, self.to_next, t, znext))
-                act(copy(origin, part, self.to_mate, t, mate))
+                act(copy(origin, part, self.to_next, at, znext))
+                act(copy(origin, part, self.to_mate, at, mate))
 
             @pl.when(ok & (self.tail | self.onward))
             def _():
-                act(copy(part, part, self.to_next, t, znext))
+                act(copy(part, part, self.to_next, at, znext))
 
             @pl.when(ok & self.member)
             def _():
-                act(copy(part, part, self.back, t, mate))
+                act(copy(part, part, self.back, at, mate))
 
         def step(self, t, ok):
-            part = rows(self.hold, block_of(t)[0])
-
-            @pl.when(ok & self.tail)
-            def _():
-                copy(part, part, self.to_mate, t, mate).wait_recv()
-
-            @pl.when(ok & self.member)
-            def _():
-                copy(part, part, self.to_next, t, mate).wait_recv()
-
-            self.sends(t, ok, lambda c: c.start())
+            for q in range(2):
+                part, at = half(self.hold, block_of(t)[0], q), 2 * t + q
+
+                @pl.when(ok & self.tail)
+                def _():
+                    copy(part, part, self.to_mate, at, mate).wait_recv()
+
+                @pl.when(ok & self.member)
+                def _():
+                    copy(part, part, self.to_next, at, mate).wait_recv()
+
+                self.sends(t, ok, lambda c: c.start(), q)
 
         def collect(self, t, ok):
-            part = rows(self.hold, block_of(t)[0])
-
-            @pl.when(ok & self.guest)
-            def _():
-                copy(part, part, self.back, t, mate).wait_recv()
+            for q in range(2):
+                part = half(self.hold, block_of(t)[0], q)
+
+                @pl.when(ok & self.guest)
+                def _():
+                    copy(part, part, self.back, 2 * t + q, mate).wait_recv()
 
     top = HeadCast(s0, sr, 0, 0, (top_mate, top_next, top_back))
     top.setup()
@@ -266,15 +270,21 @@
         def _():
             act(copy(part, part, col_back, 2 * t + way, mate))
 
-    def side_step(m):
+    held = ((zsrc >= 1) & (zsrc <= 3)).astype(jnp.int32)
+    minus_at = SIDE + 3 * (col == 1).astype(jnp.int32)
+    plus_at = minus_at + 2 * zsrc * held
+
+    def side_step(n):
+        m = n - minus_at
         full = rows(sc, block_of(m)[0])
 
         @pl.when(caster & from_zero & (m >= 0) & (m <= 15))
         def _():
             copy(full, full, col_mate, m, mate).wait_recv()
 
-        for way, (sems, far) in enumerate(((col_plus, far_plus), (col_minus, far_minus))):
-            t = m - 2 * far
+        ways = ((col_plus, far_plus, plus_at), (col_minus, far_minus, minus_at))
+        for way, (sems, far, start) in enumerate(ways):
+            t = n - start - 2 * far
             ok = (t >= 0) & (t <= 15)
             part = half(sc, block_of(t)[0], way)
 
@@ -283,6 +293,11 @@
                 copy(part, part, sems, t, mate).wait_recv()
 
             side_sends(t, ok, way, lambda c: c.start())
+
+    def side_slot(n):
+        t = n - 2 * z - 1
+        top.collect(t, top_ok(t))
+        side_step(n)
 
     def top_ok(t):
         return (t >= 0) & (t <= 15) & (block_of(t)[0] < TOP_BLOCKS)
@@ -312,9 +327,6 @@
         @pl.when((row >= 2) & ((3 * n) % 5 < 3))
         def _():
             ring((3 * n) // 5)
-
-    held = (zsrc >= 1) & (zsrc <= 3)
-    side_at = SIDE + 3 * (col == 1).astype(jnp.int32) + (LEAD - SIDE) * held.astype(jnp.int32)
 
     def lead_slot(n, carry):
         ring_slot(n)
@@ -323,9 +335,9 @@
         t = n - 2 * turns.far
         turns.step(t, turn_ok(t))
 
-        @pl.when((core == 1) & (n >= SIDE))
-        def _():
-            side_step(n - side_at)
+        @pl.when(core == 1)
+        def _():
+            side_slot(n)
 
         return carry
 
@@ -371,8 +383,10 @@
 
     def drain(t, carry):
         j, _ = block_of(t)
-        both(t, lambda c: c.wait_send())
-        top.sends(t, top_ok(t), lambda c: c.wait_send())
+        for q in range(2):
+            both(t, q, lambda c: c.wait_send())
+            top.sends(t, top_ok(t), lambda c: c.wait_send(), q)
+
 
         @pl.when(turn_ok(t))
         def _():
@@ -400,22 +414,13 @@
 
     @pl.when(core == 1)
     def _():
-        def side_slot(m, carry):
-            ring_slot(m)
-            side_step(m - side_at)
+        def later_slot(n, carry):
+            ring_slot(n)
+            side_slot(n)
             return carry
 
-        @pl.when(caster & held)
-        def _():
-            lax.fori_loop(0, 16, top_in, 0)
-
-        lax.fori_loop(LEAD, LEAD + 31, side_slot, 0)
+        lax.fori_loop(LEAD, LEAD + 31, later_slot, 0)
         lax.fori_loop(0, 16, drain, 0)
-
-        @pl.when(jnp.logical_not(caster & held))
-        def _():
-            lax.fori_loop(0, 16, top_in, 0)
-
         for c in results:
             c.wait_recv()
 
@@ -540,12 +545,14 @@
             jax.ShapeDtypeStruct((PANEL, 128), jnp.int32),
             jax.ShapeDtypeStruct((2 * NB, 2 * NB), F32),
             jax.ShapeDtypeStruct((PANEL, 2 * NB), F32),
+            jax.ShapeDtypeStruct((80, 128), F32),
         ),
         in_specs=[outside] * 3,
-        out_specs=(vmem,) * 6,
+        out_specs=(vmem,) * 7,
         scratch_shapes=[pltpu.VMEM((PANEL, PANEL), F32)] * 2
-        + [pltpu.VMEM((80, 128), F32), dma((3,))]
-        + [dma((2, 16))] * 7
+        + [dma((3,))]
+        + [dma((2, 32))] * 4
+        + [dma((2, 16))] * 3
         + [dma((2, 32))]
         + [dma((2, 2))] * 3
         + [dma((2, 3))],
@@ -581,19 +588,14 @@
     return out_c, out_s
 
 
-def finish_kernel(bins, sr, sc, s0, low, inv, load_far, dly_far, td, trail, panel, white, load, dly, sems):
-    fetch = [
-        pltpu.make_async_copy(load_far, load, sems.at[0]),
-        pltpu.make_async_copy(dly_far, dly, sems.at[1]),
-    ]
-    for c in fetch:
-        c.start()
+def finish_kernel(bins, sr, sc, s0, low, inv, load, td, dly_far, trail, panel, white, dly, sem):
+    fetch = pltpu.make_async_copy(dly_far, dly, sem)
+    fetch.start()
     row, col = lax.axis_index("row"), lax.axis_index("col")
     head = s0[:PANEL]
     mid = 2 * NB
     inv_a, inv_b = split(inv[:mid]), split(inv[mid:])
     link = split(low[...])
-    fetch[0].wait()
 
     def lanes_of(index):
         return jnp.concatenate([load[pl.ds(index * 5 + b, 1), :] for b in range(5)], axis=1)
@@ -629,7 +631,7 @@
     second = upper[mid:] - three(dot_nn, link, split(first))
     second = three(dot_nn, inv_b, split(second))
     solved = jnp.concatenate([first, second], axis=0)
-    fetch[1].wait()
+    fetch.wait()
     steer = jnp.concatenate(steer_of(dly[...], bins[0]), axis=1)
     lower = steer - three(dot_nn, own_parts, split(solved))
     padded = jnp.concatenate([solved, jnp.zeros((640 - PANEL, 256), F32)], axis=0)
@@ -639,7 +641,7 @@
     white[1] = stacked[:, 128:]
 
 
-def finish(bins, sr, sc, s0, low, inv, load, delays, td):
+def finish(bins, sr, sc, s0, low, inv, load, td, delays):
     vmem = pl.BlockSpec(memory_space=pltpu.VMEM)
     smem = pl.BlockSpec(memory_space=pltpu.SMEM)
     outside = pl.BlockSpec(memory_space=pltpu.HBM)
@@ -650,22 +652,20 @@
             jax.ShapeDtypeStruct((640, PANEL), F32),
             jax.ShapeDtypeStruct((2, 640, 128), F32),
         ),
-        in_specs=[smem] + [vmem] * 5 + [outside] * 2 + [vmem],
+        in_specs=[smem] + [vmem] * 7 + [outside],
         out_specs=(vmem,) * 3,
-        scratch_shapes=[
-            pltpu.VMEM((80, 128), F32), pltpu.VMEM((640, 128), jnp.int32), pltpu.SemaphoreType.DMA((2,)),
-        ],
+        scratch_shapes=[pltpu.VMEM((640, 128), jnp.int32), pltpu.SemaphoreType.DMA(())],
         compiler_params=pltpu.CompilerParams(vmem_limit_bytes=36 << 20),
         name="finish_tiles",
-    )(bins, sr, sc, s0, low, inv, load, delays, td)
+    )(bins, sr, sc, s0, low, inv, load, td, delays)
 
 
 def on_device(spectra, loading, delays, bin_index):
     load = pltpu.with_memory_space_constraint(loading.reshape(80, 128), pltpu.HBM)
     spectra = pltpu.with_memory_space_constraint(spectra, pltpu.HBM)
     delays = pltpu.with_memory_space_constraint(delays, pltpu.HBM)
-    sr, sc, s0, td, low, inv = gather(spectra, delays, load)
-    return finish(bin_index, sr, sc, s0, low, inv, load, delays, td)
+    sr, sc, s0, td, low, inv, lanes = gather(spectra, delays, load)
+    return finish(bin_index, sr, sc, s0, low, inv, lanes, td, delays)
 
 
 def solution(mesh):

time: 109 us -> 106 us (0.972)
  Pallas kernels: 107 us -> 105 us
    pallas_call x1, Pallas kernels: 94.4 us -> 92.2 us  [gather(): pl.pallas_call(gather_kernel, out_shape=(jax.ShapeDtypeStruct((640, 2048)...]
where the time goes in v7:
time: 106 us
  Pallas kernels  105 us (99%)
  between operations  1.45 us (1%)
    pallas_call x1, Pallas kernels, gather(): pl.pallas_call(gather_kernel, out_shape=(jax.ShapeDtypeStruct((640, 2048)...  92.2 us
    pallas_call x1, Pallas kernels, finish(): pl.pallas_call(finish_kernel, out_shape=(jax.ShapeDtypeStruct((640, 640),...  12.5 us

profile of v7, /device:TPU:177, one launch (start us, length us, event | category | flops | bytes accessed | tf_op | source)
XLA Modules:
  0.0 106.1 jit_solution(17825250985334558751)
XLA Ops:
  1.3 92.2 %gather_and_factor.1 = (bf16[640,2048]{1,0:T(8,128)(2,1)S(1)}, bf16[640,2048]{1,0:T(8,128)(2,1)S(1)}, bf16[520,2048]{1,0:T(8,128)(2,1)S(1)}, s32[512,128]{1,0:T(...) custom-call(bf16[40,2048]{1,0:T(8,128)(2,1)} %spec.1, s32[640,128]{1,0:T(8,128)} %dly_far.1, ...), custom_call_target="tpu_custom_call" | custom-call | tf_op jit(solution)/shard_map/gather_and_factor/pallas_call | solution.py:539
  93.5 12.5 %finish_tiles.1 = (f32[640,640]{1,0:T(8,128)}, f32[640,512]{1,0:T(8,128)}, f32[2,640,128]{2,1,0:T(8,128)}) custom-call(s32[1]{0:T(128)S(6)} %copy.7.bins, bf16[640,2048]{1,0:T(8,128)(2,1)S(1)} %get-tuple-element.10.sr, bf16[640,2048]{1,0:T(8,128)(2,1)S(1)} %get-tuple-element.11.sc, bf16[520,2048]{1,0:T(8,128)(2,1)S(1)} %get-tuple-element.12.s0, ...), custom_call_target="tpu_custom_call" | custom-call | tf_op jit(solution)/shard_map/finish_tiles/pallas_call | solution.py:648

commit v8 on v7

--- a/solution.py
+++ b/solution.py
@@ -294,9 +294,15 @@
 
             side_sends(t, ok, way, lambda c: c.start())
 
+    def top_in(t, carry):
+        top.collect(t, top_ok(t))
+        return carry
+
     def side_slot(n):
-        t = n - 2 * z - 1
-        top.collect(t, top_ok(t))
+        @pl.when(caster & (held == 1) & (n == plus_at))
+        def _():
+            lax.fori_loop(0, 16, top_in, 0)
+
         side_step(n)
 
     def top_ok(t):
@@ -342,10 +348,6 @@
         return carry
 
     lax.fori_loop(0, LEAD, lead_slot, 0)
-
-    def top_in(t, carry):
-        top.collect(t, top_ok(t))
-        return carry
 
     @pl.when(core == 0)
     def _():
@@ -421,6 +423,11 @@
 
         lax.fori_loop(LEAD, LEAD + 31, later_slot, 0)
         lax.fori_loop(0, 16, drain, 0)
+
+        @pl.when(jnp.logical_not(caster & (held == 1)))
+        def _():
+            lax.fori_loop(0, 16, top_in, 0)
+
         for c in results:
             c.wait_recv()
 

time: 106 us -> 106 us (level)
  no operation moved by 1% of the time
where the time goes in v8:
time: 106 us
  Pallas kernels  104 us (98%)
  between operations  1.45 us (1%)
    pallas_call x1, Pallas kernels, gather(): pl.pallas_call(gather_kernel, out_shape=(jax.ShapeDtypeStruct((640, 2048)...  91.9 us
    pallas_call x1, Pallas kernels, finish(): pl.pallas_call(finish_kernel, out_shape=(jax.ShapeDtypeStruct((640, 640),...  12.5 us

profile of v8, /device:TPU:177, one launch (start us, length us, event | category | flops | bytes accessed | tf_op | source)
XLA Modules:
  0.0 105.8 jit_solution(12188948812769727610)
XLA Ops:
  1.3 91.9 %gather_and_factor.1 = (bf16[640,2048]{1,0:T(8,128)(2,1)S(1)}, bf16[640,2048]{1,0:T(8,128)(2,1)S(1)}, bf16[520,2048]{1,0:T(8,128)(2,1)S(1)}, s32[512,128]{1,0:T(...) custom-call(bf16[40,2048]{1,0:T(8,128)(2,1)} %spec.1, s32[640,128]{1,0:T(8,128)} %dly_far.1, ...), custom_call_target="tpu_custom_call" | custom-call | tf_op jit(solution)/shard_map/gather_and_factor/pallas_call | solution.py:546
  93.2 12.5 %finish_tiles.1 = (f32[640,640]{1,0:T(8,128)}, f32[640,512]{1,0:T(8,128)}, f32[2,640,128]{2,1,0:T(8,128)}) custom-call(s32[1]{0:T(128)S(6)} %copy.7.bins, bf16[640,2048]{1,0:T(8,128)(2,1)S(1)} %get-tuple-element.10.sr, bf16[640,2048]{1,0:T(8,128)(2,1)S(1)} %get-tuple-element.11.sc, bf16[520,2048]{1,0:T(8,128)(2,1)S(1)} %get-tuple-element.12.s0, ...), custom_call_target="tpu_custom_call" | custom-call | tf_op jit(solution)/shard_map/finish_tiles/pallas_call | solution.py:655

commit v9 on v8

--- a/solution.py
+++ b/solution.py
@@ -271,7 +271,7 @@
             act(copy(part, part, col_back, 2 * t + way, mate))
 
     held = ((zsrc >= 1) & (zsrc <= 3)).astype(jnp.int32)
-    minus_at = SIDE + 3 * (col == 1).astype(jnp.int32)
+    minus_at = SIDE
     plus_at = minus_at + 2 * zsrc * held
 
     def side_step(n):
@@ -326,9 +326,9 @@
         def _():
             ring(n)
 
-        @pl.when((row == 1) & ((2 * late) % 3 < 2))
-        def _():
-            ring((2 * late) // 3)
+        @pl.when(row == 1)
+        def _():
+            ring(late)
 
         @pl.when((row >= 2) & ((3 * n) % 5 < 3))
         def _():
@@ -419,15 +419,19 @@
         def later_slot(n, carry):
             ring_slot(n)
             side_slot(n)
+
+            @pl.when((n >= LEAD + 8) & (n < LEAD + 24))
+            def _():
+                t = n - LEAD - 8
+                drain(t, 0)
+
+                @pl.when(jnp.logical_not(caster & (held == 1)))
+                def _():
+                    top.collect(t, top_ok(t))
+
             return carry
 
         lax.fori_loop(LEAD, LEAD + 31, later_slot, 0)
-        lax.fori_loop(0, 16, drain, 0)
-
-        @pl.when(jnp.logical_not(caster & (held == 1)))
-        def _():
-            lax.fori_loop(0, 16, top_in, 0)
-
         for c in results:
             c.wait_recv()
 

time: 106 us -> 104 us (0.981)
    pallas_call x1, Pallas kernels: 91.9 us -> 90.3 us  [gather(): pl.pallas_call(gather_kernel, out_shape=(jax.ShapeDtypeStruct((640, 2048)...]
where the time goes in v9:
time: 104 us
  Pallas kernels  103 us (99%)
  between operations  1.45 us (1%)
    pallas_call x1, Pallas kernels, gather(): pl.pallas_call(gather_kernel, out_shape=(jax.ShapeDtypeStruct((640, 2048)...  90.3 us
    pallas_call x1, Pallas kernels, finish(): pl.pallas_call(finish_kernel, out_shape=(jax.ShapeDtypeStruct((640, 640),...  12.5 us

profile of v9, /device:TPU:177, one launch (start us, length us, event | category | flops | bytes accessed | tf_op | source)
XLA Modules:
  0.0 104.2 jit_solution(16744003679393466836)
XLA Ops:
  1.3 90.3 %gather_and_factor.1 = (bf16[640,2048]{1,0:T(8,128)(2,1)S(1)}, bf16[640,2048]{1,0:T(8,128)(2,1)S(1)}, bf16[520,2048]{1,0:T(8,128)(2,1)S(1)}, s32[512,128]{1,0:T(...) custom-call(bf16[40,2048]{1,0:T(8,128)(2,1)} %spec.1, s32[640,128]{1,0:T(8,128)} %dly_far.1, ...), custom_call_target="tpu_custom_call" | custom-call | tf_op jit(solution)/shard_map/gather_and_factor/pallas_call | solution.py:550
  91.5 12.5 %finish_tiles.1 = (f32[640,640]{1,0:T(8,128)}, f32[640,512]{1,0:T(8,128)}, f32[2,640,128]{2,1,0:T(8,128)}) custom-call(s32[1]{0:T(128)S(6)} %copy.7.bins, bf16[640,2048]{1,0:T(8,128)(2,1)S(1)} %get-tuple-element.10.sr, bf16[640,2048]{1,0:T(8,128)(2,1)S(1)} %get-tuple-element.11.sc, bf16[520,2048]{1,0:T(8,128)(2,1)S(1)} %get-tuple-element.12.s0, ...), custom_call_target="tpu_custom_call" | custom-call | tf_op jit(solution)/shard_map/finish_tiles/pallas_call | solution.py:659
